TPU v7x, 256 devices: a whole 4x4x8 slice. The times are simulated.
256 devices in a mesh: mem: 8 (over z_lo, core), lat: 32 (over x, y, z_hi).
Axes of the slice: x: 4, y: 4, z: 8 (z_hi: 2, z_lo: 4; z = z_hi * 4 + z_lo), core: 2. Of those that a mesh axis runs over, the one named last changes fastest.
Arguments:
- members: bfloat16 [32, 4, 16, 256, 1024], P('mem', None, None, 'lat'), may hold values from -6 to 6
- increment: float32 [4, 16, 256, 1024], P(None, 'mem', 'lat'), may hold values from -6 to 6
- vertical: float32 [16, 16], replicated, may hold values from -1.5 to 1.5
- lat_taps: float32 [9], replicated, may hold values from 0.2 to 0.6
- lon_taps: float32 [9], replicated, may hold values from 0.2 to 0.6
Outputs:
- product: float32 [4, 16, 256, 1024], P(None, 'mem', 'lat')
All inputs are finite; a program needn't handle non-finite values.
Results may differ from a plain program's by a relative error of at most 0.0003.
Values sent between devices are 32-bit elements; how exact they have to be, the bound alone decides.
No kernel may reach another device: no remote copies, remote signals or barrier semaphores. Data moves between devices by JAX's collectives and lax.ppermute only.
A program may use at most 64 MiB of HBM per device.

v0:
```python
import jax
import jax.numpy as jnp
from jax import lax
from jax.sharding import PartitionSpec as P


def in_order(parts, dim):
    dims = list(parts.shape[1:])
    dims[dim] *= parts.shape[0]
    return jnp.moveaxis(parts, 0, dim).reshape(dims)


def copy_for_each(array, axis):
    count = lax.axis_size(axis)
    return lax.all_to_all(
        jnp.broadcast_to(array[None], (count, *array.shape)), axis, 0, 0, tiled=True
    )


def gathered_copies(array, axis, dim):
    return in_order(copy_for_each(array, axis), dim)


def extended(block, sides, width):
    for axis, dim in sides:
        count = lax.axis_size(axis)
        forward = [(i, i + 1) for i in range(count - 1)]
        backward = [(target, source) for source, target in forward]
        low = lax.ppermute(
            lax.slice_in_dim(block, block.shape[dim] - width, None, axis=dim), axis, forward
        )
        high = lax.ppermute(lax.slice_in_dim(block, 0, width, axis=dim), axis, backward)
        block = jnp.concatenate([low, block, high], axis=dim)
    return block


def cut_along(array, dim, count):
    dims = array.shape
    parts = array.reshape(*dims[:dim], count, dims[dim] // count, *dims[dim + 1 :])
    return jnp.moveaxis(parts, dim, 0)


def sum_at_owner(array, axis, dim):
    parts = cut_along(array, dim, lax.axis_size(axis))
    arrived = lax.all_to_all(parts, axis, split_axis=0, concat_axis=0, tiled=True)
    return arrived.sum(axis=0)


def lon_adjoint(source, kernel):
    summed = jnp.zeros(source.shape, jnp.float32)
    for offset in range(9):
        summed = summed + kernel[offset] * jnp.roll(source, offset - 4, axis=-1)
    return summed


def lon_forward(source, kernel):
    summed = jnp.zeros(source.shape, jnp.float32)
    for offset in range(9):
        summed = summed + kernel[offset] * jnp.roll(source, 4 - offset, axis=-1)
    return summed


def lat_adjoint(padded, kernel):
    row_count = padded.shape[-2] - 8
    summed = kernel[0] * padded[..., 8 : 8 + row_count, :]
    for offset in range(1, 9):
        summed = summed + kernel[offset] * padded[..., 8 - offset : 8 - offset + row_count, :]
    return summed


def lat_forward(padded, kernel):
    row_count = padded.shape[-2] - 8
    summed = kernel[0] * padded[..., 0:row_count, :]
    for offset in range(1, 9):
        summed = summed + kernel[offset] * padded[..., offset : offset + row_count, :]
    return summed


def per_device(members, increment, vertical, lat_taps, lon_taps):
    increment_all = gathered_copies(increment, "mem", 1)
    values = members.astype(jnp.float32)
    weighted = jnp.sum(values * increment_all[None], axis=1)
    weighted = lon_adjoint(weighted, lon_taps)
    weighted = jnp.einsum("kl,mkij->mlij", vertical, weighted, precision=lax.Precision.HIGHEST)
    padded = extended(weighted, (("lat", 2),), 4)
    adjoint_field = lat_adjoint(padded, lat_taps)
    padded = extended(adjoint_field, (("lat", 2),), 4)
    spread = lat_forward(padded, lat_taps)
    spread = lon_forward(spread, lon_taps)
    spread = jnp.einsum("lk,mkij->mlij", vertical, spread, precision=lax.Precision.HIGHEST)
    member_count = members.shape[0] * lax.axis_size("mem")
    member_terms = jnp.sum(values * spread[:, None], axis=0) / jnp.float32(member_count - 1)
    return sum_at_owner(member_terms, "mem", 1)


def solution(mesh):
    in_specs = (P("mem", None, None, "lat", None), P(None, "mem", "lat", None), P(), P(), P())
    out_specs = P(None, "mem", "lat", None)
    return jax.shard_map(
        per_device, mesh=mesh, in_specs=in_specs, out_specs=out_specs, check_vma=False
    )
```

profile of v0, /device:TPU:1, one launch (start us, length us, event | category | flops | bytes accessed | tf_op | source)
XLA Modules:
  0.0 370.0 jit_solution(14992672359231669511)
XLA Ops:
  0.0 2.5 broadcast_in_dim.2
  2.6 7.5 %all-to-all-start = ((f32[8,4,2,8,1024]{4,3,2,1,0:T(8,128)}), f32[8,4,2,8,1024]{4,3,2,1,0:T(8,128)S(1)}, u32[]{:S(2)}, u32[]{:S(2)}) async-start(f32[8,4,2,8,1024]{4,3,2,1,0:T(8,128)} %broadcast_in_dim.2), calls=%async_computation | async-start | bytes 4194304 | tf_op jit(solution)/shard_map/all_to_all | solution.py:15
  10.1 0.7 fusion.148
  10.8 47.4 %all-to-all-done = f32[8,4,2,8,1024]{4,3,2,1,0:T(8,128)S(1)} async-done(((f32[8,4,2,8,1024]{4,3,2,1,0:T(8,128)}), f32[8,4,2,8,1024]{4,3,2,1,0:T(8,128)S(1)}, u32[]{:S(2)}, u32[]{:S(2)}) %all-to-all-start) | async-done | bytes 2097184 | tf_op jit(solution)/shard_map/all_to_all | solution.py:15
  58.1 0.2 copy.27
  58.4 1.9 copy-done.1
  60.3 1.1 fusion
  61.4 0.8 fusion.140
  62.3 0.8 fusion.142
  63.1 0.8 fusion.144
  64.0 0.8 fusion.146
  64.9 0.2 fusion.139
  65.0 0.1 fusion.141
  65.5 1.2 copy.56
  66.7 1.2 copy.58
  67.9 1.2 copy.60
  69.1 1.2 copy.62
  70.4 1.2 copy.63
  71.6 1.4 copy.65
  73.0 1.2 copy.67
  74.2 1.2 copy.69
  75.9 12.4 %fusion.103 = f32[4,16,8,1024]{3,1,2,0:T(8,128)S(1)} fusion(f32[4,16,8,4]{3,1,2,0:T(8,128)S(1)} %copy.55, f32[4,16,8,1020]{3,1,2,0:T(8,128)S(1)} %copy.56, f32[4,16,8,3]{3,1,2,0:T(8,128)S(1)} %copy.57, f32[4,16,8,1021]{3,1,2,0:T(8,128)S(1)} %copy.58, f32[4,16,8,2]{3,1,2,0:T(8,128)S(1)} %copy.59, f32[4,16,8,1022]{3,1,2,0:T(8,128)S(1)} %copy.60, ...), kind=kOutput, calls=%fused_computation.145 | convolution fusion | flops 113770496 | bytes 20972580 | tf_op jit(solution)/shard_map/kl,mkij->mlij/dot_general | solution.py:84
  88.4 0.2 fusion.138
  88.6 1.3 collective-permute-start
  89.9 8.0 %collective-permute-start.1 = (f32[4,16,4,1024]{3,1,2,0:T(8,128)S(1)}, f32[4,16,4,1024]{3,1,2,0:T(8,128)S(1)}, u32[]{:S(2)}, u32[]{:S(2)}) collective-permute-start(f32[4,16,4,1024]{3,1,2,0:T(8,128)S(1)} %get-tuple-element.24), channel_id=1, source_target_pairs={{0,1},{1,2},{2,3},{3,4},{4,5},{5,6},{6,7},{7,8},{8,9},{9,10},{10,1... | collective-permute-start | bytes 3145736 | tf_op jit(solution)/shard_map/ppermute | solution.py:29
  97.9 0.7 fusion.147
  98.6 42.5 %collective-permute-done = f32[4,16,4,1024]{3,1,2,0:T(8,128)S(1)} collective-permute-done((f32[4,16,4,1024]{3,1,2,0:T(8,128)S(1)}, f32[4,16,4,1024]{3,1,2,0:T(8,128)S(1)}, u32[]{:S(2)}, u32[]{:S(2)}) %collective-permute-start) | collective-permute-done | bytes 1048608 | tf_op jit(solution)/shard_map/ppermute | solution.py:32
  141.1 1.2 collective-permute-done.1
  142.3 8.2 %fusion.25 = f32[4,16,8,1024]{3,1,2,0:T(8,128)S(1)} fusion(f32[4,16,8,1024]{3,1,2,0:T(8,128)S(1)} %fusion.103, f32[4,16,4,1024]{3,1,2,0:T(8,128)S(1)} %collective-permute-done.1, f32[4,16,4,1024]{3,1,2,0:T(8,128)S(1)} %collective-permute-done, f32[]{:T(128)} %bitcast.21, f32[]{:T(128)} %bitcast.20, f32[]{:T(128)} %bitcast.19, f32[]{:T(128)} %bitcast.18, ...), kind=kLoop, calls=%fused_computation.51 | loop fusion | flops 13107200 | bytes 6291492 | tf_op jit(solution)/shard_map/add | solution.py:67
  150.5 0.2 fusion.137
  150.8 27.1 %collective-permute-start.2 = (f32[4,16,4,1024]{3,1,2,0:T(8,128)S(1)}, f32[4,16,4,1024]{3,1,2,0:T(8,128)S(1)}, u32[]{:S(2)}, u32[]{:S(2)}) collective-permute-start(f32[4,16,4,1024]{3,1,2,0:T(8,128)S(1)} %get-tuple-element.21), channel_id=1, source_target_pairs={{0,1},{1,2},{2,3},{3,4},{4,5},{5,6},{6,7},{7,8},{8,9},{9,10},{10,1... | collective-permute-start | bytes 3145736 | tf_op jit(solution)/shard_map/ppermute | solution.py:29
  177.9 1.3 collective-permute-start.3
  179.2 26.8 %collective-permute-done.2 = f32[4,16,4,1024]{3,1,2,0:T(8,128)S(1)} collective-permute-done((f32[4,16,4,1024]{3,1,2,0:T(8,128)S(1)}, f32[4,16,4,1024]{3,1,2,0:T(8,128)S(1)}, u32[]{:S(2)}, u32[]{:S(2)}) %collective-permute-start.2) | collective-permute-done | bytes 1048608 | tf_op jit(solution)/shard_map/ppermute | solution.py:29
  206.0 60.7 %collective-permute-done.3 = f32[4,16,4,1024]{3,1,2,0:T(8,128)S(1)} collective-permute-done((f32[4,16,4,1024]{3,1,2,0:T(8,128)S(1)}, f32[4,16,4,1024]{3,1,2,0:T(8,128)S(1)}, u32[]{:S(2)}, u32[]{:S(2)}) %collective-permute-start.3) | collective-permute-done | bytes 1048608 | tf_op jit(solution)/shard_map/ppermute | solution.py:32
  266.7 8.3 %fusion.5 = f32[4,16,8,1024]{3,1,2,0:T(8,128)S(1)} fusion(f32[4,16,8,1024]{3,1,2,0:T(8,128)S(1)} %fusion.25, f32[4,16,4,1024]{3,1,2,0:T(8,128)S(1)} %collective-permute-done.3, f32[4,16,4,1024]{3,1,2,0:T(8,128)S(1)} %collective-permute-done.2, f32[]{:T(128)} %bitcast.21, f32[]{:T(128)} %bitcast.20, f32[]{:T(128)} %bitcast.19, f32[]{:T(128)} %bitcast.18, ...), kind=kLoop, calls=%fused_computation.31 | loop fusion | flops 13107200 | bytes 6291492 | tf_op jit(solution)/shard_map/add | solution.py:75
  275.0 0.7 fusion.131
  275.8 0.7 fusion.133
  276.5 0.7 fusion.135
  277.3 0.7 fusion.129
  278.0 0.1 fusion.132
  278.2 0.1 fusion.134
  278.6 11.8 %fusion.100 = f32[4,16,8,1024]{3,1,2,0:T(8,128)S(1)} fusion(f32[4,16,8,1020]{3,1,2,0:T(8,128)S(1)} %get-tuple-element.6, f32[4,16,8,4]{3,1,2,0:T(8,128)S(1)} %get-tuple-element.8, f32[4,16,8,1021]{3,1,2,0:T(8,128)S(1)} %get-tuple-element.10, f32[4,16,8,3]{3,1,2,0:T(8,128)S(1)} %get-tuple-element.12, f32[4,16,8,1022]{3,1,2,0:T(8,128)S(1)} %get-tuple-element.14, ...), kind=kOutput, calls=%fused_computation.144 | convolution fusion | flops 113770496 | bytes 20972580 | tf_op jit(solution)/shard_map/lk,mkij->mlij/dot_general | solution.py:90
  290.4 1.2 copy.46
  291.7 1.1 fusion.1
  292.8 0.2 broadcast_multiply_fusion
  293.0 0.2 copy.47
  293.2 75.9 %all_to_all.10 = f32[8,4,2,8,1024]{4,3,2,1,0:T(8,128)S(1)} all-to-all(f32[8,4,2,8,1024]{4,3,2,1,0:T(8,128)S(1)} %copy.47), channel_id=1, replica_groups=mesh['mem'=8,'lat'=32] {'mem'}, dimensions={0} | all-to-all | bytes 4194304 | tf_op jit(solution)/shard_map/all_to_all | solution.py:45
  369.1 0.8 reduce_sum.29
  (19 shorter events, 1.0 us)
Async XLA Ops:
  0.0 75.9 %copy-start = (f32[16,16]{1,0:T(8,128)S(1)}, f32[16,16]{1,0:T(8,128)}, u32[]{:S(2)}) copy-start(f32[16,16]{1,0:T(8,128)} %param.7) | copy-start | bytes 3076
  2.6 7.5 %copy-start.2 = (f32[9]{0:T(128)S(1)}, f32[9]{0:T(128)}, u32[]{:S(2)}) copy-start(f32[9]{0:T(128)} %param.9) | copy-start | bytes 112
  2.6 55.6 %all-to-all-start = ((f32[8,4,2,8,1024]{4,3,2,1,0:T(8,128)}), f32[8,4,2,8,1024]{4,3,2,1,0:T(8,128)S(1)}, u32[]{:S(2)}, u32[]{:S(2)}) async-start(f32[8,4,2,8,1024]{4,3,2,1,0:T(8,128)} %broadcast_in_dim.2), calls=%async_computation | async-start | bytes 4194304 | tf_op jit(solution)/shard_map/all_to_all | solution.py:15
  58.1 2.2 copy-start.1
  88.3 9.5 %copy-start.3 = (f32[9]{0:T(128)S(1)}, f32[9]{0:T(128)}, u32[]{:S(2)}) copy-start(f32[9]{0:T(128)} %param.8) | copy-start | bytes 112
  88.6 52.5 %collective-permute-start = (f32[4,16,4,1024]{3,1,2,0:T(8,128)S(1)}, f32[4,16,4,1024]{3,1,2,0:T(8,128)S(1)}, u32[]{:S(2)}, u32[]{:S(2)}) collective-permute-start(f32[4,16,4,1024]{3,1,2,0:T(8,128)S(1)} %get-tuple-element.23), channel_id=1, source_target_pairs={{1,0},{2,1},{3,2},{4,3},{5,4},{6,5},{7,6},{8,7},{9,8},{10,9},{11,1... | collective-permute-start | bytes 3145736 | tf_op jit(solution)/shard_map/ppermute | solution.py:32
  89.9 52.4 %collective-permute-start.1 = (f32[4,16,4,1024]{3,1,2,0:T(8,128)S(1)}, f32[4,16,4,1024]{3,1,2,0:T(8,128)S(1)}, u32[]{:S(2)}, u32[]{:S(2)}) collective-permute-start(f32[4,16,4,1024]{3,1,2,0:T(8,128)S(1)} %get-tuple-element.24), channel_id=1, source_target_pairs={{0,1},{1,2},{2,3},{3,4},{4,5},{5,6},{6,7},{7,8},{8,9},{9,10},{10,1... | collective-permute-start | bytes 3145736 | tf_op jit(solution)/shard_map/ppermute | solution.py:29
  150.8 55.3 %collective-permute-start.2 = (f32[4,16,4,1024]{3,1,2,0:T(8,128)S(1)}, f32[4,16,4,1024]{3,1,2,0:T(8,128)S(1)}, u32[]{:S(2)}, u32[]{:S(2)}) collective-permute-start(f32[4,16,4,1024]{3,1,2,0:T(8,128)S(1)} %get-tuple-element.21), channel_id=1, source_target_pairs={{0,1},{1,2},{2,3},{3,4},{4,5},{5,6},{6,7},{7,8},{8,9},{9,10},{10,1... | collective-permute-start | bytes 3145736 | tf_op jit(solution)/shard_map/ppermute | solution.py:29
  177.9 88.8 %collective-permute-start.3 = (f32[4,16,4,1024]{3,1,2,0:T(8,128)S(1)}, f32[4,16,4,1024]{3,1,2,0:T(8,128)S(1)}, u32[]{:S(2)}, u32[]{:S(2)}) collective-permute-start(f32[4,16,4,1024]{3,1,2,0:T(8,128)S(1)} %get-tuple-element.22), channel_id=1, source_target_pairs={{1,0},{2,1},{3,2},{4,3},{5,4},{6,5},{7,6},{8,7},{9,8},{10,9},{11,1... | collective-permute-start | bytes 3145736 | tf_op jit(solution)/shard_map/ppermute | solution.py:32
where the time goes:
time: 371 us; the launch traced here: 370 us
  waiting for transfers between devices  179 us (48%)
  blocking collectives  75.9 us (20%)
  starting transfers between devices  45.2 us (12%)
  local copies, waits for them, and re-layouts  25.9 us (7%)
  matrix products  24.2 us (7%)
  other arithmetic  19.8 us (5%)
    ppermute x2, waiting for transfers between devices, extended(): lax.ppermute(lax.slice_in_dim(block, 0, width, axis=dim), axis, backward)  103 us
    all_to_all x1, blocking collectives, sum_at_owner(): lax.all_to_all(parts, axis, split_axis=0, concat_axis=0, tiled=True)  75.9 us
    all_to_all x1, waiting for transfers between devices, copy_for_each(): lax.all_to_all(jnp.broadcast_to(array[None], (count, *array.shape)), axis...  47.4 us
    ppermute x2, starting transfers between devices, extended(): lax.ppermute(lax.slice_in_dim(block, block.shape[dim] - width, None, axis...  35.1 us
    ppermute x2, waiting for transfers between devices, extended(): lax.ppermute(lax.slice_in_dim(block, block.shape[dim] - width, None, axis...  28 us
    dot_general x1, matrix products, per_device(): jnp.einsum('kl,mkij->mlij', vertical, weighted, precision=lax.Precision.H...  12.4 us
    unnamed x24, local copies, waits for them, and re-layouts  12.3 us
    dot_general x1, matrix products, per_device(): jnp.einsum('lk,mkij->mlij', vertical, spread, precision=lax.Precision.HIG...  11.8 us
  transfers between devices with their start and end apart: 5, of which 5 were waited for; matrix products, arithmetic and copies ran while one was open for 0% of the time, Pallas kernels for 0%

commit v1 on v0

v1 whole, which is shorter than its diff:
```python
import functools

import jax
import jax.numpy as jnp
from jax import lax
from jax.experimental import pallas as pl
from jax.experimental.pallas import tpu as pltpu
from jax.sharding import PartitionSpec as P


WIDTHS = (384, 384, 256)
STARTS = tuple(sum(WIDTHS[:i]) for i in range(len(WIDTHS)))
LEVELS = 16
ROWS = 8
LON = 1024
VARS = 4
LOCAL = 4
CHIPS = 4
FLAT = LEVELS * ROWS
CHIP_ROWS = FLAT // CHIPS
PAIR = 2 * ROWS
SIDE = 128
BLOCK = 256
WINDOW = BLOCK + 2 * SIDE
HIGHEST = lax.Precision.HIGHEST


def split(value):
    high = value.astype(jnp.bfloat16)
    low = (value - high.astype(jnp.float32)).astype(jnp.bfloat16)
    return high, low


def dot(a, b, precision=None):
    return jnp.dot(a, b, preferred_element_type=jnp.float32, precision=precision)


def iotas(*shape):
    return (
        lax.broadcasted_iota(jnp.int32, shape, 0),
        lax.broadcasted_iota(jnp.int32, shape, 1),
    )


def where_one(mask):
    return jnp.where(mask, jnp.float32(1), jnp.float32(0))


def diagonals(distance, values):
    filled = jnp.zeros(distance.shape, jnp.float32)
    for at, value in values:
        filled = jnp.where(distance == at, value, filled)
    return filled


def prepare_kernel(slabs, place, lat_taps, lon_taps, vertical, band_high, band_low, mix):
    chip, core, slab = place[0], place[1], place[2]
    lon = [lon_taps[i] for i in range(9)]
    lat = [lat_taps[i] for i in range(9)]
    square = []
    for shift in range(9):
        terms = [lon[i] * lon[i + shift] for i in range(9 - shift)]
        square.append(functools.reduce(lambda a, b: a + b, terms))
    row, col = iotas(WINDOW, BLOCK)
    distance = jnp.abs(row - SIDE - col)
    band_high[...], band_low[...] = split(diagonals(distance, list(enumerate(square))))

    row, col = iotas(16, 24)
    adjoint = diagonals(row + 8 - col, list(enumerate(lat)))
    line = slab * ROWS - 4 + row
    adjoint = jnp.where((line >= 0) & (line < slabs * ROWS), adjoint, 0.0)
    row, col = iotas(ROWS, 16)
    forward = diagonals(col - row, list(enumerate(lat)))
    band = dot(forward, adjoint, HIGHEST)

    row, col = iotas(LEVELS, LEVELS)
    step, side = row // 4, (row // 2) % 2
    level = 4 * lax.rem(chip - step + CHIPS, CHIPS) + 2 * lax.rem(core + side, 2) + row % 2
    ordered = dot(where_one(level == col), vertical[...], HIGHEST)
    square = lax.dot_general(
        ordered, ordered, (((1,), (1,)), ((), ())), precision=HIGHEST,
        preferred_element_type=jnp.float32,
    )
    row, col = iotas(FLAT, LEVELS)
    tall = where_one(row // ROWS == col)
    row, col = iotas(LEVELS, 3 * FLAT)
    wide = where_one((col % FLAT) // ROWS == row)
    levels = dot(dot(tall, square, HIGHEST), wide, HIGHEST)
    row, col = iotas(FLAT, ROWS)
    tall = where_one(row % ROWS == col)
    row, col = iotas(24, 3 * FLAT)
    odd = lax.rem(slab, 2)
    which = jnp.where(col < FLAT, 1, jnp.where(col < 2 * FLAT, 2 - 2 * odd, 2 * odd))
    wide = where_one(which * ROWS + col % ROWS == row)
    rows = dot(dot(tall, band, HIGHEST), wide, HIGHEST)
    mix[:FLAT], mix[FLAT:] = split(levels * rows)


def prepare(slabs, place, lat_taps, lon_taps, vertical):
    smem = pl.BlockSpec(memory_space=pltpu.SMEM)
    return pl.pallas_call(
        functools.partial(prepare_kernel, slabs),
        out_shape=[
            jax.ShapeDtypeStruct((WINDOW, BLOCK), jnp.bfloat16),
            jax.ShapeDtypeStruct((WINDOW, BLOCK), jnp.bfloat16),
            jax.ShapeDtypeStruct((2 * FLAT, 3 * FLAT), jnp.bfloat16),
        ],
        in_specs=[smem, smem, smem] + whole(1),
        out_specs=whole(3),
        cost_estimate=pl.CostEstimate(flops=1 << 24, bytes_accessed=1 << 20, transcendentals=0),
        name="prepare",
    )(place, lat_taps, lon_taps, vertical)


def whole(count):
    return [pl.BlockSpec(memory_space=pltpu.VMEM)] * count


def weigh_kernel(steps, starts, place, members, *refs):
    chip, core = place[0], place[1]
    count = len(steps)
    parts, (band_high, band_low) = refs[: 2 * count], refs[2 * count : 2 * count + 2]
    outs, both = refs[2 * count + 2 : -1], refs[-1]
    rows_of_one = count * CHIP_ROWS
    rows = LOCAL * rows_of_one

    def member(m, carry):
        for i, step in enumerate(steps):
            for side in range(2):
                part = parts[2 * i + side]
                level = 4 * lax.rem(chip - step + CHIPS, CHIPS) + 2 * lax.rem(core + side, 2)
                total = members[m, 0, pl.ds(level, 2)].astype(jnp.float32) * part[0]
                for v in range(1, VARS):
                    total += members[m, v, pl.ds(level, 2)].astype(jnp.float32) * part[v]
                first = m * rows_of_one + i * CHIP_ROWS + side * PAIR
                for base, value in zip((0, rows), split(total.reshape(PAIR, LON))):
                    line = pl.ds(pl.multiple_of(base + first, PAIR), PAIR)
                    both[line, SIDE : SIDE + LON] = value
                    both[line, :SIDE] = value[:, LON - SIDE :]
                    both[line, SIDE + LON :] = value[:, :SIDE]
        return carry

    lax.fori_loop(0, LOCAL, member, 0)
    for block in range(LON // BLOCK):
        cols = slice(block * BLOCK, block * BLOCK + WINDOW)
        wide = dot(both[:, cols], band_high[...])
        total = wide[:rows] + wide[rows:] + dot(both[:rows, cols], band_low[...])
        total = total.reshape(LOCAL, rows_of_one, BLOCK)
        for half in range(2):
            where = block * BLOCK + half * SIDE
            out = max(i for i in range(len(starts)) if starts[i] <= where)
            to = where - starts[out]
            outs[out][:, :, to : to + SIDE] = total[:, :, half * SIDE : (half + 1) * SIDE]


def weigh(steps, widths, place, members, parts, band):
    starts = tuple(sum(widths[:i]) for i in range(len(widths)))
    rows = len(steps) * CHIP_ROWS
    return pl.pallas_call(
        functools.partial(weigh_kernel, steps, starts),
        out_shape=[jax.ShapeDtypeStruct((LOCAL, rows, w), jnp.float32) for w in widths],
        in_specs=[pl.BlockSpec(memory_space=pltpu.SMEM)] + whole(3 + len(parts)),
        out_specs=whole(len(widths)),
        scratch_shapes=[pltpu.VMEM((2 * LOCAL * rows, LON + 2 * SIDE), jnp.bfloat16)],
        cost_estimate=pl.CostEstimate(
            flops=len(steps) << 28, bytes_accessed=len(steps) << 21, transcendentals=0
        ),
    )(place, members, *parts, *band)


def spread_kernel(start, width, place, members, *refs):
    near, far = refs[:3], refs[3:6]
    mix, keep, give = refs[6], refs[7 : 7 + CHIPS], refs[7 + CHIPS]
    high_ref, low_ref, spread_ref = refs[8 + CHIPS :]
    cols = slice(start, start + width)

    def member(m, carry):
        for at in range(3):
            lines = slice(at * FLAT, at * FLAT + CHIP_ROWS)
            high_ref[lines], low_ref[lines] = split(near[at][m, :, cols])
            lines = slice(at * FLAT + CHIP_ROWS, (at + 1) * FLAT)
            high_ref[lines], low_ref[lines] = split(far[at][m])
        both = dot(mix[...], high_ref[...])
        spread_ref[m] = both[:FLAT] + both[FLAT:] + dot(mix[:FLAT], low_ref[...])
        return carry

    lax.fori_loop(0, LOCAL, member, 0)
    chip, core = place[0], place[1]
    for step in range(CHIPS):
        to = (CHIPS - step) % CHIPS
        for side in range(2):
            first = step * CHIP_ROWS + side * PAIR
            level = 4 * lax.rem(chip - step + CHIPS, CHIPS) + 2 * lax.rem(core + side, 2)
            out = give.at[to] if side else keep[to]
            for v in range(VARS):
                total = None
                for m in range(LOCAL):
                    rows = spread_ref[m, first : first + PAIR].reshape(2, ROWS, width)
                    term = members[m, v, pl.ds(level, 2), :, cols].astype(jnp.float32) * rows
                    total = term if total is None else total + term
                out[v] = total


def spread_product(start, width, place, members, near, far, mix):
    part = jax.ShapeDtypeStruct((VARS, 2, ROWS, width), jnp.float32)
    return pl.pallas_call(
        functools.partial(spread_kernel, start, width),
        out_shape=[part] * CHIPS + [jax.ShapeDtypeStruct((CHIPS, *part.shape), jnp.float32)],
        in_specs=[pl.BlockSpec(memory_space=pltpu.SMEM)] + whole(8),
        out_specs=whole(CHIPS + 1),
        scratch_shapes=[pltpu.VMEM((3 * FLAT, width), jnp.bfloat16)] * 2
        + [pltpu.VMEM((LOCAL, FLAT, width), jnp.float32)],
        cost_estimate=pl.CostEstimate(
            flops=width << 20, bytes_accessed=width * 12 << 10, transcendentals=0
        ),
    )(place, members, *near, *far, mix)


def fold_kernel(*refs):
    keep, got, outs = refs[:CHIPS], refs[CHIPS], refs[CHIPS + 1 :]
    for to in range(CHIPS):
        outs[to][...] = keep[to][...] + got[to]


def fold(keep, got):
    return pl.pallas_call(
        fold_kernel,
        out_shape=[jax.ShapeDtypeStruct(k.shape, k.dtype) for k in keep],
        in_specs=whole(CHIPS + 1),
        out_specs=whole(CHIPS),
        cost_estimate=pl.CostEstimate(flops=got.size, bytes_accessed=12 * got.size, transcendentals=0),
        name="fold",
    )(*keep, got)


def per_device(members, increment, vertical, lat_taps, lon_taps):
    mem, lat = lax.axis_index("mem"), lax.axis_index("lat")
    slabs = lax.axis_size("lat")
    count = LOCAL * lax.axis_size("mem")
    swap_core = [(i, i ^ 1) for i in range(2 * CHIPS)]
    along = lambda step: [(i, (i + 2 * step) % (2 * CHIPS)) for i in range(2 * CHIPS)]
    swap_lat = [(i, i ^ 1) for i in range(slabs)]
    pass_on = [(i, i + 2) for i in range(0, slabs - 2, 2)] + [(i, i - 2) for i in range(3, slabs, 2)]

    held = [increment] + [lax.ppermute(increment, "mem", along(step)) for step in (1, 2, 3)]
    other = [lax.ppermute(part, "mem", swap_core) for part in held]
    index = jnp.arange(3)
    place = jnp.where(index == 0, mem // 2, jnp.where(index == 1, mem % 2, lat)).astype(jnp.int32)
    *band, mix = prepare(slabs, place, lat_taps, lon_taps, vertical)

    (near,) = weigh((0,), (LON,), place, members, [held[0], other[0]], band)
    near = [near, lax.ppermute(near, "lat", swap_lat)]
    near.append(lax.ppermute(near[1], "lat", pass_on))

    parts = [part[step] for step in (1, 2, 3) for part in (held, other)]
    fields = weigh((1, 2, 3), WIDTHS, place, members, parts, band)
    across = [lax.ppermute(field, "lat", swap_lat) for field in fields]
    finals = []
    for i, (start, width) in enumerate(zip(STARTS, WIDTHS)):
        beyond = lax.ppermute(across[i], "lat", pass_on)
        *keep, give = spread_product(
            start, width, place, members, near, [fields[i], across[i], beyond], mix
        )
        got = lax.ppermute(give, "mem", swap_core)
        both = fold(keep, got)
        final = both[0]
        for step in (1, 2, 3):
            final = final + lax.ppermute(both[step], "mem", along(step))
        finals.append(final)
    return jnp.concatenate(finals, axis=-1) / jnp.float32(count - 1)


def solution(mesh):
    in_specs = (P("mem", None, None, "lat", None), P(None, "mem", "lat", None), P(), P(), P())
    out_specs = P(None, "mem", "lat", None)
    return jax.shard_map(
        per_device, mesh=mesh, in_specs=in_specs, out_specs=out_specs, check_vma=False
    )
```

time: 371 us -> 196 us (0.53)
  waiting for transfers between devices: 179 us -> 96.7 us
  blocking collectives: 75.9 us -> 0 us
  Pallas kernels: 0 us -> 34.6 us
  matrix products: 24.2 us -> 0 us
  local copies, waits for them, and re-layouts: 25.9 us -> 5.48 us
  other arithmetic: 19.8 us -> 3.9 us
  starting transfers between devices: 45.2 us -> 51.6 us
    all_to_all x1 -> x0, blocking collectives: 75.9 us -> none  [sum_at_owner(): lax.all_to_all(parts, axis, split_axis=0, concat_axis=0, tiled=True)]
    all_to_all x1 -> x0, waiting for transfers between devices: 47.4 us -> none  [copy_for_each(): lax.all_to_all(jnp.broadcast_to(array[None], (count, *array.shape)), axis...]
    pallas_call x0 -> x9, Pallas kernels: none -> 34.6 us  [the longest x3 16 us: spread_product(): pl.pallas_call(functools.partial(spread_kernel, start, width), out_shape=...]
    ppermute x4 -> x27, waiting for transfers between devices: 131 us -> 96.7 us  [the longest x3 46.7 us: per_device(): across = [lax.ppermute(field, 'lat', swap_lat) for field in fields]]
    dot_general x2 -> x0, matrix products: 24.2 us -> none  [the longest x1 12.4 us: per_device(): jnp.einsum('kl,mkij->mlij', vertical, weighted, precision=lax.Precision.H...]
    ppermute x4 -> x27, starting transfers between devices: 37.7 us -> 51.6 us  [the longest x9 10.9 us: per_device(): final = final + lax.ppermute(both[step], 'mem', along(step))]
    add x2 -> x3, other arithmetic: 16.5 us -> 2.7 us  [per_device(): final = final + lax.ppermute(both[step], 'mem', along(step))]
    slice x20 -> x0, local copies, waits for them, and re-layouts: 9.34 us -> none  [the longest x9 4.23 us: lon_forward(): summed = summed + kernel[offset] * jnp.roll(source, 4 - offset, axis=-1)]
  transfers between devices with their start and end apart: 5 -> 27, of which waited for: 5 -> 10; matrix products, arithmetic and copies ran while one was open for 0% -> 1% of each run, Pallas kernels for 0% -> 18%
where the time goes in v1:
time: 196 us; the launch traced here: 192 us
  waiting for transfers between devices  96.7 us (49%)
  starting transfers between devices  51.6 us (26%)
  Pallas kernels  34.6 us (18%)
  local copies, waits for them, and re-layouts  5.48 us (3%)
  other arithmetic  3.9 us (2%)
    ppermute x3, waiting for transfers between devices, per_device(): across = [lax.ppermute(field, 'lat', swap_lat) for field in fields]  46.7 us
    ppermute x1, waiting for transfers between devices, per_device(): near = [near, lax.ppermute(near, 'lat', swap_lat)]  24.6 us
    ppermute x3, waiting for transfers between devices, per_device(): lax.ppermute(increment, 'mem', along(step))  18.1 us
    pallas_call x3, Pallas kernels, spread_product(): pl.pallas_call(functools.partial(spread_kernel, start, width), out_shape=...  16 us
    ppermute x9, starting transfers between devices, per_device(): final = final + lax.ppermute(both[step], 'mem', along(step))  10.9 us
    ppermute x3, starting transfers between devices, per_device(): across = [lax.ppermute(field, 'lat', swap_lat) for field in fields]  10.6 us
    ppermute x3, starting transfers between devices, per_device(): beyond = lax.ppermute(across[i], 'lat', pass_on)  10.4 us
    pallas_call x2, Pallas kernels, weigh(): pl.pallas_call(functools.partial(weigh_kernel, steps, starts), out_shape=...  10 us
  transfers between devices with their start and end apart: 27, of which 10 were waited for; matrix products, arithmetic and copies ran while one was open for 1% of the time, Pallas kernels for 18%

profile of v1, /device:TPU:1, one launch (start us, length us, event | category | flops | bytes accessed | tf_op | source)
XLA Modules:
  0.0 192.4 jit_solution(16175356502410588098)
XLA Ops:
  0.0 2.5 %collective-permute-start.3 = (f32[4,2,8,1024]{3,2,1,0:T(8,128)}, f32[4,2,8,1024]{3,2,1,0:T(8,128)S(1)}, u32[]{:S(2)}, u32[]{:S(2)}) collective-permute-start(f32[4,2,8,1024]{3,2,1,0:T(8,128)} %refs_0_.1), channel_id=1, source_target_pairs={{0,64},{32,96},{64,128},{96,160},{128,192},{160,224},{192,0},{224,... | collective-permute-start | bytes 786440 | tf_op jit(solution)/shard_map/ppermute | solution.py:245
  2.5 2.7 %collective-permute-start.7 = (f32[4,2,8,1024]{3,2,1,0:T(8,128)}, f32[4,2,8,1024]{3,2,1,0:T(8,128)S(1)}, u32[]{:S(2)}, u32[]{:S(2)}) collective-permute-start(f32[4,2,8,1024]{3,2,1,0:T(8,128)} %refs_0_.1), channel_id=1, source_target_pairs={{0,192},{32,224},{64,0},{96,32},{128,64},{160,96},{192,128},{224,1... | collective-permute-start | bytes 786440 | tf_op jit(solution)/shard_map/ppermute | solution.py:245
  5.5 5.1 %collective-permute-done.3.refs_0_ = f32[4,2,8,1024]{3,2,1,0:T(8,128)S(1)} collective-permute-done((f32[4,2,8,1024]{3,2,1,0:T(8,128)}, f32[4,2,8,1024]{3,2,1,0:T(8,128)S(1)}, u32[]{:S(2)}, u32[]{:S(2)}) %collective-permute-start.3) | collective-permute-done | bytes 262176 | tf_op jit(solution)/shard_map/ppermute | solution.py:245
  10.5 3.9 %collective-permute-start.4 = (f32[4,2,8,1024]{3,2,1,0:T(8,128)S(1)}, f32[4,2,8,1024]{3,2,1,0:T(8,128)S(1)}, u32[]{:S(2)}, u32[]{:S(2)}) collective-permute-start(f32[4,2,8,1024]{3,2,1,0:T(8,128)S(1)} %collective-permute-done.3.refs_0_), channel_id=1, source_target_pairs={{0,32},{32,0},{64,96},{96,64},{128,160},{160,128},{192,224},{224,1... | collective-permute-start | bytes 786440 | tf_op jit(solution)/shard_map/ppermute | solution.py:246
  14.4 1.2 collective-permute-done.7.refs_4_
  15.7 1.5 collective-permute-start.8
  17.2 11.8 %collective-permute-done.5.refs_2_ = f32[4,2,8,1024]{3,2,1,0:T(8,128)S(1)} collective-permute-done((f32[4,2,8,1024]{3,2,1,0:T(8,128)}, f32[4,2,8,1024]{3,2,1,0:T(8,128)S(1)}, u32[]{:S(2)}, u32[]{:S(2)}) %collective-permute-start.5) | collective-permute-done | bytes 262176 | tf_op jit(solution)/shard_map/ppermute | solution.py:245
  29.0 0.5 collective-permute-start.6
  30.0 2.9 %prepare.1 = (bf16[512,256]{1,0:T(8,128)(2,1)}, bf16[512,256]{1,0:T(8,128)(2,1)}, bf16[256,384]{1,0:T(8,128)(2,1)}) custom-call(s32[3]{0:T(128)} %compare_select_fusion.1.place, f32[9]{0:T(128)} %lat_taps.1, f32[9]{0:T(128)} %lon_taps.1, f32[16,16]{1,0:T(8,128)} %vertical.1), custom_call_target="tpu_custom_call" | custom-call | flops 16777216 | bytes 1048576 | tf_op jit(solution)/shard_map/prepare/pallas_call | solution.py:101
  32.9 0.6 copy-done.12
  33.7 5.9 %shard_map.56 = (f32[4,96,384]{2,1,0:T(8,128)}, f32[4,96,384]{2,1,0:T(8,128)}, f32[4,96,256]{2,1,0:T(8,128)}) custom-call(s32[3]{0:T(128)} %compare_select_fusion.1.place, bf16[4,4,16,8,1024]{4,3,2,1,0:T(8,128)(2,1)} %members.9, f32[4,2,8,1024]{3,2,1,0:T(8,128)} %copy-done.9, f32[4,2,8,1024]{3,2,1,0:T(8,128)} %copy-done.12, f32[4,2,8,1024]{3,2,1,0:T(8,128)} %copy-done.11, ...), custom_call_target="tpu_custom_call" | custom-call | flops 805306368 | bytes 6291456 | tf_op jit(solution)/shard_map/pallas_call | solution.py:159
  39.6 5.2 %collective-permute-start.9 = (f32[4,96,384]{2,1,0:T(8,128)}, f32[4,96,384]{2,1,0:T(8,128)S(1)}, u32[]{:S(2)}, u32[]{:S(2)}) collective-permute-start(f32[4,96,384]{2,1,0:T(8,128)} %get-tuple-element.40.refs_3_), channel_id=1, source_target_pairs={{0,1},{1,0},{2,3},{3,2},{4,5},{5,4},{6,7},{7,6},{8,9},{9,8},{10,11... | collective-permute-start | bytes 1769480 | tf_op jit(solution)/shard_map/ppermute | solution.py:257
  44.8 0.7 copy-done.14
  45.5 4.1 %shard_map.55.refs_0_ = f32[4,32,1024]{2,1,0:T(8,128)} custom-call(s32[3]{0:T(128)} %compare_select_fusion.1.place, bf16[4,4,16,8,1024]{4,3,2,1,0:T(8,128)(2,1)} %members.9, f32[4,2,8,1024]{3,2,1,0:T(8,128)} %refs_0_.1, f32[4,2,8,1024]{3,2,1,0:T(8,128)} %copy-done.14, bf16[512,256]{1,0:T(8,128)(2,1)} %get-tuple-element.38.refs_2_.refs_6_, ...), custom_call_target="tpu_custom_call" | custom-call | flops 268435456 | bytes 2097152 | tf_op jit(solution)/shard_map/pallas_call | solution.py:159
  49.8 5.2 %collective-permute-start.15 = (f32[4,96,384]{2,1,0:T(8,128)S(1)}, f32[4,96,384]{2,1,0:T(8,128)S(1)}, u32[]{:S(2)}, u32[]{:S(2)}) collective-permute-start(f32[4,96,384]{2,1,0:T(8,128)S(1)} %copy-done.2), channel_id=1, source_target_pairs={{0,1},{1,0},{2,3},{3,2},{4,5},{5,4},{6,7},{7,6},{8,9},{9,8},{10,11... | collective-permute-start | bytes 1769480 | tf_op jit(solution)/shard_map/ppermute | solution.py:257
  55.2 18.2 %collective-permute-done.9.refs_4_ = f32[4,96,384]{2,1,0:T(8,128)S(1)} collective-permute-done((f32[4,96,384]{2,1,0:T(8,128)}, f32[4,96,384]{2,1,0:T(8,128)S(1)}, u32[]{:S(2)}, u32[]{:S(2)}) %collective-permute-start.9) | collective-permute-done | bytes 589856 | tf_op jit(solution)/shard_map/ppermute | solution.py:257
  73.4 3.2 %collective-permute-start.10 = (f32[4,96,384]{2,1,0:T(8,128)S(1)}, f32[4,96,384]{2,1,0:T(8,128)S(1)}, u32[]{:S(2)}, u32[]{:S(2)}) collective-permute-start(f32[4,96,384]{2,1,0:T(8,128)S(1)} %collective-permute-done.9.refs_4_), channel_id=1, source_target_pairs={{0,2},{2,4},{4,6},{6,8},{8,10},{10,12},{12,14},{14,16},{16,18},{18... | collective-permute-start | bytes 1769480 | tf_op jit(solution)/shard_map/ppermute | solution.py:260
  76.6 24.6 %collective-permute-done.1.refs_1_ = f32[4,32,1024]{2,1,0:T(8,128)S(1)} collective-permute-done((f32[4,32,1024]{2,1,0:T(8,128)}, f32[4,32,1024]{2,1,0:T(8,128)S(1)}, u32[]{:S(2)}, u32[]{:S(2)}) %collective-permute-start.1) | collective-permute-done | bytes 524320 | tf_op jit(solution)/shard_map/ppermute | solution.py:252
  101.2 3.2 %collective-permute-start.2 = (f32[4,32,1024]{2,1,0:T(8,128)S(1)}, f32[4,32,1024]{2,1,0:T(8,128)S(1)}, u32[]{:S(2)}, u32[]{:S(2)}) collective-permute-start(f32[4,32,1024]{2,1,0:T(8,128)S(1)} %collective-permute-done.1.refs_1_), channel_id=1, source_target_pairs={{0,2},{2,4},{4,6},{6,8},{8,10},{10,12},{12,14},{14,16},{16,18},{18... | collective-permute-start | bytes 1572872 | tf_op jit(solution)/shard_map/ppermute | solution.py:253
  104.4 23.2 %collective-permute-done.15.refs_4_ = f32[4,96,384]{2,1,0:T(8,128)S(1)} collective-permute-done((f32[4,96,384]{2,1,0:T(8,128)S(1)}, f32[4,96,384]{2,1,0:T(8,128)S(1)}, u32[]{:S(2)}, u32[]{:S(2)}) %collective-permute-start.15) | collective-permute-done | bytes 589856 | tf_op jit(solution)/shard_map/ppermute | solution.py:257
  127.6 3.2 %collective-permute-start.16 = (f32[4,96,384]{2,1,0:T(8,128)S(1)}, f32[4,96,384]{2,1,0:T(8,128)S(1)}, u32[]{:S(2)}, u32[]{:S(2)}) collective-permute-start(f32[4,96,384]{2,1,0:T(8,128)S(1)} %collective-permute-done.15.refs_4_), channel_id=1, source_target_pairs={{0,2},{2,4},{4,6},{6,8},{8,10},{10,12},{12,14},{14,16},{16,18},{18... | collective-permute-start | bytes 1769480 | tf_op jit(solution)/shard_map/ppermute | solution.py:260
  130.8 5.3 %collective-permute-done.21.refs_4_ = f32[4,96,256]{2,1,0:T(8,128)} collective-permute-done((f32[4,96,256]{2,1,0:T(8,128)}, f32[4,96,256]{2,1,0:T(8,128)}, u32[]{:S(2)}, u32[]{:S(2)}) %collective-permute-start.21) | collective-permute-done | bytes 393248 | tf_op jit(solution)/shard_map/ppermute | solution.py:257
  136.1 4.0 %collective-permute-start.22 = (f32[4,96,256]{2,1,0:T(8,128)}, f32[4,96,256]{2,1,0:T(8,128)}, u32[]{:S(2)}, u32[]{:S(2)}) collective-permute-start(f32[4,96,256]{2,1,0:T(8,128)} %collective-permute-done.21.refs_4_), channel_id=1, source_target_pairs={{0,2},{2,4},{4,6},{6,8},{8,10},{10,12},{12,14},{14,16},{16,18},{18... | collective-permute-start | bytes 1179656 | tf_op jit(solution)/shard_map/ppermute | solution.py:260
  140.1 0.8 copy-done.1
  141.1 5.6 %shard_map.57 = (f32[4,2,8,384]{3,2,1,0:T(8,128)}, f32[4,2,8,384]{3,2,1,0:T(8,128)}, f32[4,2,8,384]{3,2,1,0:T(8,128)}, f32[4,2,8,384]{3,2,1,0:T(8,128)}, f32[4,4,2,8,384]{4,3,2,1,0:T(8,128)}) custom-call(s32[3]{0:T(128)} %compare_select_fusion.1.place, bf16[4,4,16,8,1024]{4,3,2,1,0:T(8,128)(2,1)} %members.9, f32[4,32,1024]{2,1,0:T(8,128)} %shard_map.55.refs_0_, ...), custom_call_target="tpu_custom_call" | custom-call | flops 402653184 | bytes 4718592 | tf_op jit(solution)/shard_map/pallas_call | solution.py:206
  146.6 1.7 collective-permute-start.11
  148.3 1.3 collective-permute-done.22.refs_5_
  149.6 4.9 %shard_map.59 = (f32[4,2,8,256]{3,2,1,0:T(8,128)}, f32[4,2,8,256]{3,2,1,0:T(8,128)}, f32[4,2,8,256]{3,2,1,0:T(8,128)}, f32[4,2,8,256]{3,2,1,0:T(8,128)}, f32[4,4,2,8,256]{4,3,2,1,0:T(8,128)}) custom-call(s32[3]{0:T(128)} %compare_select_fusion.1.place, bf16[4,4,16,8,1024]{4,3,2,1,0:T(8,128)(2,1)} %members.9, f32[4,32,1024]{2,1,0:T(8,128)} %shard_map.55.refs_0_, ...), custom_call_target="tpu_custom_call" | custom-call | flops 268435456 | bytes 3145728 | tf_op jit(solution)/shard_map/pallas_call | solution.py:206
  154.5 3.2 %collective-permute-start.23 = (f32[4,4,2,8,256]{4,3,2,1,0:T(8,128)}, f32[4,4,2,8,256]{4,3,2,1,0:T(8,128)S(1)}, u32[]{:S(2)}, u32[]{:S(2)}) collective-permute-start(f32[4,4,2,8,256]{4,3,2,1,0:T(8,128)} %get-tuple-element.66), channel_id=1, source_target_pairs={{0,32},{32,0},{64,96},{96,64},{128,160},{160,128},{192,224},{224,1... | collective-permute-start | bytes 786440 | tf_op jit(solution)/shard_map/ppermute | solution.py:264
  157.7 0.8 copy-done.5
  158.6 5.5 %shard_map.58 = (f32[4,2,8,384]{3,2,1,0:T(8,128)}, f32[4,2,8,384]{3,2,1,0:T(8,128)}, f32[4,2,8,384]{3,2,1,0:T(8,128)}, f32[4,2,8,384]{3,2,1,0:T(8,128)}, f32[4,4,2,8,384]{4,3,2,1,0:T(8,128)}) custom-call(s32[3]{0:T(128)} %compare_select_fusion.1.place, bf16[4,4,16,8,1024]{4,3,2,1,0:T(8,128)(2,1)} %members.9, f32[4,32,1024]{2,1,0:T(8,128)} %shard_map.55.refs_0_, ...), custom_call_target="tpu_custom_call" | custom-call | flops 402653184 | bytes 4718592 | tf_op jit(solution)/shard_map/pallas_call | solution.py:206
  164.1 0.7 copy-done.16
  164.8 1.8 fold.5
  166.6 1.1 collective-permute-start.25
  167.8 2.1 %collective-permute-start.26 = (f32[4,2,8,256]{3,2,1,0:T(8,128)}, f32[4,2,8,256]{3,2,1,0:T(8,128)S(1)}, u32[]{:S(2)}, u32[]{:S(2)}) collective-permute-start(f32[4,2,8,256]{3,2,1,0:T(8,128)} %get-tuple-element.70), channel_id=1, source_target_pairs={{0,192},{32,224},{64,0},{96,32},{128,64},{160,96},{192,128},{224,1... | collective-permute-start | bytes 196616 | tf_op jit(solution)/shard_map/ppermute | solution.py:268
  169.9 0.7 copy-done.8
  170.7 2.0 %fold.3 = (f32[4,2,8,384]{3,2,1,0:T(8,128)}, f32[4,2,8,384]{3,2,1,0:T(8,128)}, f32[4,2,8,384]{3,2,1,0:T(8,128)}, f32[4,2,8,384]{3,2,1,0:T(8,128)}) custom-call(f32[4,2,8,384]{3,2,1,0:T(8,128)} %get-tuple-element.42.refs_0_, f32[4,2,8,384]{3,2,1,0:T(8,128)} %get-tuple-element.43.refs_1_, f32[4,2,8,384]{3,2,1,0:T(8,128)} %get-tuple-element.44.refs_2_, ...), custom_call_target="tpu_custom_call" | custom-call | flops 98304 | bytes 1179648 | tf_op jit(solution)/shard_map/fold/pallas_call | solution.py:226
  172.9 1.3 collective-permute-start.13
  174.2 2.9 %collective-permute-start.14 = (f32[4,2,8,384]{3,2,1,0:T(8,128)}, f32[4,2,8,384]{3,2,1,0:T(8,128)S(1)}, u32[]{:S(2)}, u32[]{:S(2)}) collective-permute-start(f32[4,2,8,384]{3,2,1,0:T(8,128)} %get-tuple-element.50), channel_id=1, source_target_pairs={{0,192},{32,224},{64,0},{96,32},{128,64},{160,96},{192,128},{224,1... | collective-permute-start | bytes 294920 | tf_op jit(solution)/shard_map/ppermute | solution.py:268
  177.0 0.9 add_add_fusion.2
  177.9 0.7 copy-done.7
  178.6 1.9 %fold.4 = (f32[4,2,8,384]{3,2,1,0:T(8,128)}, f32[4,2,8,384]{3,2,1,0:T(8,128)}, f32[4,2,8,384]{3,2,1,0:T(8,128)}, f32[4,2,8,384]{3,2,1,0:T(8,128)}) custom-call(f32[4,2,8,384]{3,2,1,0:T(8,128)} %get-tuple-element.52.refs_0_, f32[4,2,8,384]{3,2,1,0:T(8,128)} %get-tuple-element.53.refs_1_, f32[4,2,8,384]{3,2,1,0:T(8,128)} %get-tuple-element.54.refs_2_, ...), custom_call_target="tpu_custom_call" | custom-call | flops 98304 | bytes 1179648 | tf_op jit(solution)/shard_map/fold/pallas_call | solution.py:226
  181.0 2.9 %collective-permute-start.20 = (f32[4,2,8,384]{3,2,1,0:T(8,128)}, f32[4,2,8,384]{3,2,1,0:T(8,128)S(1)}, u32[]{:S(2)}, u32[]{:S(2)}) collective-permute-start(f32[4,2,8,384]{3,2,1,0:T(8,128)} %get-tuple-element.60), channel_id=1, source_target_pairs={{0,192},{32,224},{64,0},{96,32},{128,64},{160,96},{192,128},{224,1... | collective-permute-start | bytes 294920 | tf_op jit(solution)/shard_map/ppermute | solution.py:268
  183.8 0.9 add_add_fusion.1
  184.8 1.5 collective-permute-done.18
  186.2 4.5 %collective-permute-done.19 = f32[4,2,8,384]{3,2,1,0:T(8,128)S(1)} collective-permute-done((f32[4,2,8,384]{3,2,1,0:T(8,128)}, f32[4,2,8,384]{3,2,1,0:T(8,128)S(1)}, u32[]{:S(2)}, u32[]{:S(2)}) %collective-permute-start.19) | collective-permute-done | bytes 98336 | tf_op jit(solution)/shard_map/ppermute | solution.py:268
  190.8 0.9 add_add_fusion
  191.7 0.7 maximum_multiply_fusion
  (54 shorter events, 2.2 us)
Async XLA Ops:
  0.0 10.5 %collective-permute-start.3 = (f32[4,2,8,1024]{3,2,1,0:T(8,128)}, f32[4,2,8,1024]{3,2,1,0:T(8,128)S(1)}, u32[]{:S(2)}, u32[]{:S(2)}) collective-permute-start(f32[4,2,8,1024]{3,2,1,0:T(8,128)} %refs_0_.1), channel_id=1, source_target_pairs={{0,64},{32,96},{64,128},{96,160},{128,192},{160,224},{192,0},{224,... | collective-permute-start | bytes 786440 | tf_op jit(solution)/shard_map/ppermute | solution.py:245
  2.5 13.2 %collective-permute-start.7 = (f32[4,2,8,1024]{3,2,1,0:T(8,128)}, f32[4,2,8,1024]{3,2,1,0:T(8,128)S(1)}, u32[]{:S(2)}, u32[]{:S(2)}) collective-permute-start(f32[4,2,8,1024]{3,2,1,0:T(8,128)} %refs_0_.1), channel_id=1, source_target_pairs={{0,192},{32,224},{64,0},{96,32},{128,64},{160,96},{192,128},{224,1... | collective-permute-start | bytes 786440 | tf_op jit(solution)/shard_map/ppermute | solution.py:245
  5.2 23.8 %collective-permute-start.5 = (f32[4,2,8,1024]{3,2,1,0:T(8,128)}, f32[4,2,8,1024]{3,2,1,0:T(8,128)S(1)}, u32[]{:S(2)}, u32[]{:S(2)}) collective-permute-start(f32[4,2,8,1024]{3,2,1,0:T(8,128)} %refs_0_.1), channel_id=1, source_target_pairs={{0,128},{32,160},{64,192},{96,224},{128,0},{160,32},{192,64},{224,... | collective-permute-start | bytes 786440 | tf_op jit(solution)/shard_map/ppermute | solution.py:245
  10.5 22.4 %copy-start.9 = (f32[4,2,8,1024]{3,2,1,0:T(8,128)}, f32[4,2,8,1024]{3,2,1,0:T(8,128)S(1)}, u32[]{:S(2)}) copy-start(f32[4,2,8,1024]{3,2,1,0:T(8,128)S(1)} %collective-permute-done.3.refs_0_) | copy-start | bytes 786436
  10.5 22.3 %collective-permute-start.4 = (f32[4,2,8,1024]{3,2,1,0:T(8,128)S(1)}, f32[4,2,8,1024]{3,2,1,0:T(8,128)S(1)}, u32[]{:S(2)}, u32[]{:S(2)}) collective-permute-start(f32[4,2,8,1024]{3,2,1,0:T(8,128)S(1)} %collective-permute-done.3.refs_0_), channel_id=1, source_target_pairs={{0,32},{32,0},{64,96},{96,64},{128,160},{160,128},{192,224},{224,1... | collective-permute-start | bytes 786440 | tf_op jit(solution)/shard_map/ppermute | solution.py:246
  15.7 17.2 %copy-start.10 = (f32[4,2,8,1024]{3,2,1,0:T(8,128)}, f32[4,2,8,1024]{3,2,1,0:T(8,128)S(1)}, u32[]{:S(2)}) copy-start(f32[4,2,8,1024]{3,2,1,0:T(8,128)S(1)} %collective-permute-done.7.refs_4_) | copy-start | bytes 786436
  15.7 17.2 %collective-permute-start.8 = (f32[4,2,8,1024]{3,2,1,0:T(8,128)S(1)}, f32[4,2,8,1024]{3,2,1,0:T(8,128)S(1)}, u32[]{:S(2)}, u32[]{:S(2)}) collective-permute-start(f32[4,2,8,1024]{3,2,1,0:T(8,128)S(1)} %collective-permute-done.7.refs_4_), channel_id=1, source_target_pairs={{0,32},{32,0},{64,96},{96,64},{128,160},{160,128},{192,224},{224,1... | collective-permute-start | bytes 786440 | tf_op jit(solution)/shard_map/ppermute | solution.py:246
  29.0 3.9 %copy-start.11 = (f32[4,2,8,1024]{3,2,1,0:T(8,128)}, f32[4,2,8,1024]{3,2,1,0:T(8,128)S(1)}, u32[]{:S(2)}) copy-start(f32[4,2,8,1024]{3,2,1,0:T(8,128)S(1)} %collective-permute-done.5.refs_2_) | copy-start | bytes 786436
  29.0 3.9 %collective-permute-start.6 = (f32[4,2,8,1024]{3,2,1,0:T(8,128)S(1)}, f32[4,2,8,1024]{3,2,1,0:T(8,128)S(1)}, u32[]{:S(2)}, u32[]{:S(2)}) collective-permute-start(f32[4,2,8,1024]{3,2,1,0:T(8,128)S(1)} %collective-permute-done.5.refs_2_), channel_id=1, source_target_pairs={{0,32},{32,0},{64,96},{96,64},{128,160},{160,128},{192,224},{224,1... | collective-permute-start | bytes 786440 | tf_op jit(solution)/shard_map/ppermute | solution.py:246
  29.5 15.4 %collective-permute-start = (f32[4,2,8,1024]{3,2,1,0:T(8,128)}, f32[4,2,8,1024]{3,2,1,0:T(8,128)S(1)}, u32[]{:S(2)}, u32[]{:S(2)}) collective-permute-start(f32[4,2,8,1024]{3,2,1,0:T(8,128)} %refs_0_.1), channel_id=1, source_target_pairs={{0,32},{32,0},{64,96},{96,64},{128,160},{160,128},{192,224},{224,1... | collective-permute-start | bytes 786440 | tf_op jit(solution)/shard_map/ppermute | solution.py:246
  32.9 0.7 copy-start.12
  32.9 0.8 copy-start.13
  32.9 0.8 copy-start.15
  39.6 10.2 %copy-start.2 = (f32[4,96,384]{2,1,0:T(8,128)S(1)}, f32[4,96,384]{2,1,0:T(8,128)}, u32[]{:S(2)}) copy-start(f32[4,96,384]{2,1,0:T(8,128)} %get-tuple-element.51.refs_3_) | copy-start | bytes 1769476
  39.6 33.8 %collective-permute-start.9 = (f32[4,96,384]{2,1,0:T(8,128)}, f32[4,96,384]{2,1,0:T(8,128)S(1)}, u32[]{:S(2)}, u32[]{:S(2)}) collective-permute-start(f32[4,96,384]{2,1,0:T(8,128)} %get-tuple-element.40.refs_3_), channel_id=1, source_target_pairs={{0,1},{1,0},{2,3},{3,2},{4,5},{5,4},{6,7},{7,6},{8,9},{9,8},{10,11... | collective-permute-start | bytes 1769480 | tf_op jit(solution)/shard_map/ppermute | solution.py:257
  44.8 0.7 copy-start.14
  49.7 51.5 %collective-permute-start.1 = (f32[4,32,1024]{2,1,0:T(8,128)}, f32[4,32,1024]{2,1,0:T(8,128)S(1)}, u32[]{:S(2)}, u32[]{:S(2)}) collective-permute-start(f32[4,32,1024]{2,1,0:T(8,128)} %shard_map.55.refs_0_), channel_id=1, source_target_pairs={{0,1},{1,0},{2,3},{3,2},{4,5},{5,4},{6,7},{7,6},{8,9},{9,8},{10,11... | collective-permute-start | bytes 1572872 | tf_op jit(solution)/shard_map/ppermute | solution.py:252
  49.8 77.8 %collective-permute-start.15 = (f32[4,96,384]{2,1,0:T(8,128)S(1)}, f32[4,96,384]{2,1,0:T(8,128)S(1)}, u32[]{:S(2)}, u32[]{:S(2)}) collective-permute-start(f32[4,96,384]{2,1,0:T(8,128)S(1)} %copy-done.2), channel_id=1, source_target_pairs={{0,1},{1,0},{2,3},{3,2},{4,5},{5,4},{6,7},{7,6},{8,9},{9,8},{10,11... | collective-permute-start | bytes 1769480 | tf_op jit(solution)/shard_map/ppermute | solution.py:257
  55.0 81.1 %collective-permute-start.21 = (f32[4,96,256]{2,1,0:T(8,128)}, f32[4,96,256]{2,1,0:T(8,128)}, u32[]{:S(2)}, u32[]{:S(2)}) collective-permute-start(f32[4,96,256]{2,1,0:T(8,128)} %get-tuple-element.61.refs_3_), channel_id=1, source_target_pairs={{0,1},{1,0},{2,3},{3,2},{4,5},{5,4},{6,7},{7,6},{8,9},{9,8},{10,11... | collective-permute-start | bytes 1179656 | tf_op jit(solution)/shard_map/ppermute | solution.py:257
  73.4 66.7 %copy-start.4 = (f32[4,96,384]{2,1,0:T(8,128)}, f32[4,96,384]{2,1,0:T(8,128)S(1)}, u32[]{:S(2)}) copy-start(f32[4,96,384]{2,1,0:T(8,128)S(1)} %collective-permute-done.9.refs_4_) | copy-start | bytes 1769476
  73.4 66.7 %collective-permute-start.10 = (f32[4,96,384]{2,1,0:T(8,128)S(1)}, f32[4,96,384]{2,1,0:T(8,128)S(1)}, u32[]{:S(2)}, u32[]{:S(2)}) collective-permute-start(f32[4,96,384]{2,1,0:T(8,128)S(1)} %collective-permute-done.9.refs_4_), channel_id=1, source_target_pairs={{0,2},{2,4},{4,6},{6,8},{8,10},{10,12},{12,14},{14,16},{16,18},{18... | collective-permute-start | bytes 1769480 | tf_op jit(solution)/shard_map/ppermute | solution.py:260
  101.2 38.9 %copy-start = (f32[4,32,1024]{2,1,0:T(8,128)}, f32[4,32,1024]{2,1,0:T(8,128)S(1)}, u32[]{:S(2)}) copy-start(f32[4,32,1024]{2,1,0:T(8,128)S(1)} %collective-permute-done.1.refs_1_) | copy-start | bytes 1572868
  101.2 38.9 %collective-permute-start.2 = (f32[4,32,1024]{2,1,0:T(8,128)S(1)}, f32[4,32,1024]{2,1,0:T(8,128)S(1)}, u32[]{:S(2)}, u32[]{:S(2)}) collective-permute-start(f32[4,32,1024]{2,1,0:T(8,128)S(1)} %collective-permute-done.1.refs_1_), channel_id=1, source_target_pairs={{0,2},{2,4},{4,6},{6,8},{8,10},{10,12},{12,14},{14,16},{16,18},{18... | collective-permute-start | bytes 1572872 | tf_op jit(solution)/shard_map/ppermute | solution.py:253
  127.6 30.2 %copy-start.3 = (f32[4,96,384]{2,1,0:T(8,128)}, f32[4,96,384]{2,1,0:T(8,128)S(1)}, u32[]{:S(2)}) copy-start(f32[4,96,384]{2,1,0:T(8,128)S(1)} %collective-permute-done.15.refs_4_) | copy-start | bytes 1769476
  127.6 30.2 %collective-permute-start.16 = (f32[4,96,384]{2,1,0:T(8,128)S(1)}, f32[4,96,384]{2,1,0:T(8,128)S(1)}, u32[]{:S(2)}, u32[]{:S(2)}) collective-permute-start(f32[4,96,384]{2,1,0:T(8,128)S(1)} %collective-permute-done.15.refs_4_), channel_id=1, source_target_pairs={{0,2},{2,4},{4,6},{6,8},{8,10},{10,12},{12,14},{14,16},{16,18},{18... | collective-permute-start | bytes 1769480 | tf_op jit(solution)/shard_map/ppermute | solution.py:260
  136.1 13.5 %collective-permute-start.22 = (f32[4,96,256]{2,1,0:T(8,128)}, f32[4,96,256]{2,1,0:T(8,128)}, u32[]{:S(2)}, u32[]{:S(2)}) collective-permute-start(f32[4,96,256]{2,1,0:T(8,128)} %collective-permute-done.21.refs_4_), channel_id=1, source_target_pairs={{0,2},{2,4},{4,6},{6,8},{8,10},{10,12},{12,14},{14,16},{16,18},{18... | collective-permute-start | bytes 1179656 | tf_op jit(solution)/shard_map/ppermute | solution.py:260
  140.1 0.8 copy-start.1
  140.1 1.0 copy-start.6
  146.6 23.3 %collective-permute-start.11 = (f32[4,4,2,8,384]{4,3,2,1,0:T(8,128)}, f32[4,4,2,8,384]{4,3,2,1,0:T(8,128)S(1)}, u32[]{:S(2)}, u32[]{:S(2)}) collective-permute-start(f32[4,4,2,8,384]{4,3,2,1,0:T(8,128)} %get-tuple-element.46), channel_id=1, source_target_pairs={{0,32},{32,0},{64,96},{96,64},{128,160},{160,128},{192,224},{224,1... | collective-permute-start | bytes 1179656 | tf_op jit(solution)/shard_map/ppermute | solution.py:264
  154.5 9.6 %collective-permute-start.23 = (f32[4,4,2,8,256]{4,3,2,1,0:T(8,128)}, f32[4,4,2,8,256]{4,3,2,1,0:T(8,128)S(1)}, u32[]{:S(2)}, u32[]{:S(2)}) collective-permute-start(f32[4,4,2,8,256]{4,3,2,1,0:T(8,128)} %get-tuple-element.66), channel_id=1, source_target_pairs={{0,32},{32,0},{64,96},{96,64},{128,160},{160,128},{192,224},{224,1... | collective-permute-start | bytes 786440 | tf_op jit(solution)/shard_map/ppermute | solution.py:264
  157.7 0.8 copy-start.5
  164.1 13.8 %collective-permute-start.17 = (f32[4,4,2,8,384]{4,3,2,1,0:T(8,128)}, f32[4,4,2,8,384]{4,3,2,1,0:T(8,128)S(1)}, u32[]{:S(2)}, u32[]{:S(2)}) collective-permute-start(f32[4,4,2,8,384]{4,3,2,1,0:T(8,128)} %get-tuple-element.56), channel_id=1, source_target_pairs={{0,32},{32,0},{64,96},{96,64},{128,160},{160,128},{192,224},{224,1... | collective-permute-start | bytes 1179656 | tf_op jit(solution)/shard_map/ppermute | solution.py:264
  164.1 0.7 copy-start.16
  166.6 6.3 %collective-permute-start.24 = (f32[4,2,8,256]{3,2,1,0:T(8,128)}, f32[4,2,8,256]{3,2,1,0:T(8,128)S(1)}, u32[]{:S(2)}, u32[]{:S(2)}) collective-permute-start(f32[4,2,8,256]{3,2,1,0:T(8,128)} %get-tuple-element.68), channel_id=1, source_target_pairs={{0,64},{32,96},{64,128},{96,160},{128,192},{160,224},{192,0},{224,... | collective-permute-start | bytes 196616 | tf_op jit(solution)/shard_map/ppermute | solution.py:268
  166.6 7.5 %collective-permute-start.25 = (f32[4,2,8,256]{3,2,1,0:T(8,128)}, f32[4,2,8,256]{3,2,1,0:T(8,128)S(1)}, u32[]{:S(2)}, u32[]{:S(2)}) collective-permute-start(f32[4,2,8,256]{3,2,1,0:T(8,128)} %get-tuple-element.69), channel_id=1, source_target_pairs={{0,128},{32,160},{64,192},{96,224},{128,0},{160,32},{192,64},{224,... | collective-permute-start | bytes 196616 | tf_op jit(solution)/shard_map/ppermute | solution.py:268
  167.8 9.3 %collective-permute-start.26 = (f32[4,2,8,256]{3,2,1,0:T(8,128)}, f32[4,2,8,256]{3,2,1,0:T(8,128)S(1)}, u32[]{:S(2)}, u32[]{:S(2)}) collective-permute-start(f32[4,2,8,256]{3,2,1,0:T(8,128)} %get-tuple-element.70), channel_id=1, source_target_pairs={{0,192},{32,224},{64,0},{96,32},{128,64},{160,96},{192,128},{224,1... | collective-permute-start | bytes 196616 | tf_op jit(solution)/shard_map/ppermute | solution.py:268
  169.9 0.7 copy-start.8
  172.6 8.3 %collective-permute-start.12 = (f32[4,2,8,384]{3,2,1,0:T(8,128)}, f32[4,2,8,384]{3,2,1,0:T(8,128)S(1)}, u32[]{:S(2)}, u32[]{:S(2)}) collective-permute-start(f32[4,2,8,384]{3,2,1,0:T(8,128)} %get-tuple-element.48), channel_id=1, source_target_pairs={{0,64},{32,96},{64,128},{96,160},{128,192},{160,224},{192,0},{224,... | collective-permute-start | bytes 294920 | tf_op jit(solution)/shard_map/ppermute | solution.py:268
  172.9 10.9 %collective-permute-start.13 = (f32[4,2,8,384]{3,2,1,0:T(8,128)}, f32[4,2,8,384]{3,2,1,0:T(8,128)S(1)}, u32[]{:S(2)}, u32[]{:S(2)}) collective-permute-start(f32[4,2,8,384]{3,2,1,0:T(8,128)} %get-tuple-element.49), channel_id=1, source_target_pairs={{0,128},{32,160},{64,192},{96,224},{128,0},{160,32},{192,64},{224,... | collective-permute-start | bytes 294920 | tf_op jit(solution)/shard_map/ppermute | solution.py:268
  174.2 9.7 %collective-permute-start.14 = (f32[4,2,8,384]{3,2,1,0:T(8,128)}, f32[4,2,8,384]{3,2,1,0:T(8,128)S(1)}, u32[]{:S(2)}, u32[]{:S(2)}) collective-permute-start(f32[4,2,8,384]{3,2,1,0:T(8,128)} %get-tuple-element.50), channel_id=1, source_target_pairs={{0,192},{32,224},{64,0},{96,32},{128,64},{160,96},{192,128},{224,1... | collective-permute-start | bytes 294920 | tf_op jit(solution)/shard_map/ppermute | solution.py:268
  177.9 0.7 copy-start.7
  180.6 5.7 %collective-permute-start.18 = (f32[4,2,8,384]{3,2,1,0:T(8,128)}, f32[4,2,8,384]{3,2,1,0:T(8,128)S(1)}, u32[]{:S(2)}, u32[]{:S(2)}) collective-permute-start(f32[4,2,8,384]{3,2,1,0:T(8,128)} %get-tuple-element.58), channel_id=1, source_target_pairs={{0,64},{32,96},{64,128},{96,160},{128,192},{160,224},{192,0},{224,... | collective-permute-start | bytes 294920 | tf_op jit(solution)/shard_map/ppermute | solution.py:268
  180.6 10.2 %collective-permute-start.19 = (f32[4,2,8,384]{3,2,1,0:T(8,128)}, f32[4,2,8,384]{3,2,1,0:T(8,128)S(1)}, u32[]{:S(2)}, u32[]{:S(2)}) collective-permute-start(f32[4,2,8,384]{3,2,1,0:T(8,128)} %get-tuple-element.59), channel_id=1, source_target_pairs={{0,128},{32,160},{64,192},{96,224},{128,0},{160,32},{192,64},{224,... | collective-permute-start | bytes 294920 | tf_op jit(solution)/shard_map/ppermute | solution.py:268
  181.0 9.8 %collective-permute-start.20 = (f32[4,2,8,384]{3,2,1,0:T(8,128)}, f32[4,2,8,384]{3,2,1,0:T(8,128)S(1)}, u32[]{:S(2)}, u32[]{:S(2)}) collective-permute-start(f32[4,2,8,384]{3,2,1,0:T(8,128)} %get-tuple-element.60), channel_id=1, source_target_pairs={{0,192},{32,224},{64,0},{96,32},{128,64},{160,96},{192,128},{224,1... | collective-permute-start | bytes 294920 | tf_op jit(solution)/shard_map/ppermute | solution.py:268

commit v2 on v1

--- a/solution.py
+++ b/solution.py
@@ -22,6 +22,7 @@
 SIDE = 128
 BLOCK = 256
 WINDOW = BLOCK + 2 * SIDE
+GRANT = 24 << 20
 HIGHEST = lax.Precision.HIGHEST
 
 
@@ -101,12 +102,13 @@
     return pl.pallas_call(
         functools.partial(prepare_kernel, slabs),
         out_shape=[
-            jax.ShapeDtypeStruct((WINDOW, BLOCK), jnp.bfloat16),
-            jax.ShapeDtypeStruct((WINDOW, BLOCK), jnp.bfloat16),
-            jax.ShapeDtypeStruct((2 * FLAT, 3 * FLAT), jnp.bfloat16),
+            pltpu.VMEM((WINDOW, BLOCK), jnp.bfloat16),
+            pltpu.VMEM((WINDOW, BLOCK), jnp.bfloat16),
+            pltpu.VMEM((2 * FLAT, 3 * FLAT), jnp.bfloat16),
         ],
         in_specs=[smem, smem, smem] + whole(1),
         out_specs=whole(3),
+        compiler_params=pltpu.CompilerParams(vmem_limit_bytes=GRANT),
         cost_estimate=pl.CostEstimate(flops=1 << 24, bytes_accessed=1 << 20, transcendentals=0),
         name="prepare",
     )(place, lat_taps, lon_taps, vertical)
@@ -114,6 +116,10 @@
 
 def whole(count):
     return [pl.BlockSpec(memory_space=pltpu.VMEM)] * count
+
+
+def near_core(*arrays):
+    return [pltpu.with_memory_space_constraint(a, pltpu.VMEM) for a in arrays]
 
 
 def weigh_kernel(steps, starts, place, members, *refs):
@@ -158,14 +164,15 @@
     rows = len(steps) * CHIP_ROWS
     return pl.pallas_call(
         functools.partial(weigh_kernel, steps, starts),
-        out_shape=[jax.ShapeDtypeStruct((LOCAL, rows, w), jnp.float32) for w in widths],
+        out_shape=[pltpu.VMEM((LOCAL, rows, w), jnp.float32) for w in widths],
         in_specs=[pl.BlockSpec(memory_space=pltpu.SMEM)] + whole(3 + len(parts)),
         out_specs=whole(len(widths)),
         scratch_shapes=[pltpu.VMEM((2 * LOCAL * rows, LON + 2 * SIDE), jnp.bfloat16)],
+        compiler_params=pltpu.CompilerParams(vmem_limit_bytes=GRANT),
         cost_estimate=pl.CostEstimate(
             flops=len(steps) << 28, bytes_accessed=len(steps) << 21, transcendentals=0
         ),
-    )(place, members, *parts, *band)
+    )(place, *near_core(members, *parts, *band))
 
 
 def spread_kernel(start, width, place, members, *refs):
@@ -202,18 +209,19 @@
 
 
 def spread_product(start, width, place, members, near, far, mix):
-    part = jax.ShapeDtypeStruct((VARS, 2, ROWS, width), jnp.float32)
+    shape = (VARS, 2, ROWS, width)
     return pl.pallas_call(
         functools.partial(spread_kernel, start, width),
-        out_shape=[part] * CHIPS + [jax.ShapeDtypeStruct((CHIPS, *part.shape), jnp.float32)],
+        out_shape=[pltpu.VMEM(shape, jnp.float32)] * CHIPS + [pltpu.VMEM((CHIPS, *shape), jnp.float32)],
         in_specs=[pl.BlockSpec(memory_space=pltpu.SMEM)] + whole(8),
         out_specs=whole(CHIPS + 1),
         scratch_shapes=[pltpu.VMEM((3 * FLAT, width), jnp.bfloat16)] * 2
         + [pltpu.VMEM((LOCAL, FLAT, width), jnp.float32)],
+        compiler_params=pltpu.CompilerParams(vmem_limit_bytes=GRANT),
         cost_estimate=pl.CostEstimate(
             flops=width << 20, bytes_accessed=width * 12 << 10, transcendentals=0
         ),
-    )(place, members, *near, *far, mix)
+    )(place, *near_core(members, *near, *far, mix))
 
 
 def fold_kernel(*refs):
@@ -225,12 +233,13 @@
 def fold(keep, got):
     return pl.pallas_call(
         fold_kernel,
-        out_shape=[jax.ShapeDtypeStruct(k.shape, k.dtype) for k in keep],
+        out_shape=[pltpu.VMEM(k.shape, k.dtype) for k in keep],
         in_specs=whole(CHIPS + 1),
         out_specs=whole(CHIPS),
+        compiler_params=pltpu.CompilerParams(vmem_limit_bytes=GRANT),
         cost_estimate=pl.CostEstimate(flops=got.size, bytes_accessed=12 * got.size, transcendentals=0),
         name="fold",
-    )(*keep, got)
+    )(*near_core(*keep, got))
 
 
 def per_device(members, increment, vertical, lat_taps, lon_taps):

time: 196 us -> 184 us (0.939)
  Pallas kernels: 34.6 us -> 12.5 us
  waiting for transfers between devices: 96.7 us -> 109 us
  other arithmetic: 3.9 us -> 0.8 us
  starting transfers between devices: 51.6 us -> 54.1 us
    pallas_call x3, Pallas kernels: 16 us -> 6.23 us  [spread_product(): pl.pallas_call(functools.partial(spread_kernel, start, width), out_shape=...]
    pallas_call x4, Pallas kernels: 8.56 us -> 1.98 us  [the longest x1 1.87 us: prepare(): pl.pallas_call(functools.partial(prepare_kernel, slabs), out_shape=[pltpu...]
    pallas_call x2, Pallas kernels: 10 us -> 4.25 us  [weigh(): pl.pallas_call(functools.partial(weigh_kernel, steps, starts), out_shape=...]
    ppermute x3, waiting for transfers between devices: 1.32 us -> 6.23 us  [per_device(): beyond = lax.ppermute(across[i], 'lat', pass_on)]
    ppermute x9, waiting for transfers between devices: 6.01 us -> 10 us  [per_device(): final = final + lax.ppermute(both[step], 'mem', along(step))]
    ppermute x3, waiting for transfers between devices: 46.7 us -> 49.6 us  [per_device(): across = [lax.ppermute(field, 'lat', swap_lat) for field in fields]]
    add x3, other arithmetic: 2.7 us -> 0.07 us  [per_device(): final = final + lax.ppermute(both[step], 'mem', along(step))]
    ppermute x9, starting transfers between devices: 10.9 us -> 13.5 us  [per_device(): final = final + lax.ppermute(both[step], 'mem', along(step))]
  transfers between devices with their start and end apart: 27 -> 27, of which waited for: 10 -> 11; matrix products, arithmetic and copies ran while one was open for 1% -> 0% of each run, Pallas kernels for 18% -> 7%
where the time goes in v2:
time: 184 us; the launch traced here: 180 us
  waiting for transfers between devices  109 us (59%)
  starting transfers between devices  54.1 us (29%)
  Pallas kernels  12.5 us (7%)
  local copies, waits for them, and re-layouts  4.2 us (2%)
    ppermute x3, waiting for transfers between devices, per_device(): across = [lax.ppermute(field, 'lat', swap_lat) for field in fields]  49.6 us
    ppermute x1, waiting for transfers between devices, per_device(): near = [near, lax.ppermute(near, 'lat', swap_lat)]  24.5 us
    ppermute x3, waiting for transfers between devices, per_device(): lax.ppermute(increment, 'mem', along(step))  18.1 us
    ppermute x9, starting transfers between devices, per_device(): final = final + lax.ppermute(both[step], 'mem', along(step))  13.5 us
    ppermute x3, starting transfers between devices, per_device(): across = [lax.ppermute(field, 'lat', swap_lat) for field in fields]  10.7 us
    ppermute x9, waiting for transfers between devices, per_device(): final = final + lax.ppermute(both[step], 'mem', along(step))  10 us
    ppermute x3, starting transfers between devices, per_device(): beyond = lax.ppermute(across[i], 'lat', pass_on)  9.73 us
    ppermute x3, waiting for transfers between devices, per_device(): beyond = lax.ppermute(across[i], 'lat', pass_on)  6.23 us
  transfers between devices with their start and end apart: 27, of which 11 were waited for; matrix products, arithmetic and copies ran while one was open for 0% of the time, Pallas kernels for 7%

profile of v2, /device:TPU:1, one launch (start us, length us, event | category | flops | bytes accessed | tf_op | source)
XLA Modules:
  0.0 180.3 jit_solution(13522828632455863973)
XLA Ops:
  0.0 2.5 %collective-permute-start.3 = (f32[4,2,8,1024]{3,2,1,0:T(8,128)}, f32[4,2,8,1024]{3,2,1,0:T(8,128)S(1)}, u32[]{:S(2)}, u32[]{:S(2)}) collective-permute-start(f32[4,2,8,1024]{3,2,1,0:T(8,128)} %refs_0_.1), channel_id=1, source_target_pairs={{0,64},{32,96},{64,128},{96,160},{128,192},{160,224},{192,0},{224,... | collective-permute-start | bytes 786440 | tf_op jit(solution)/shard_map/ppermute | solution.py:254
  2.5 2.7 %collective-permute-start.7 = (f32[4,2,8,1024]{3,2,1,0:T(8,128)}, f32[4,2,8,1024]{3,2,1,0:T(8,128)S(1)}, u32[]{:S(2)}, u32[]{:S(2)}) collective-permute-start(f32[4,2,8,1024]{3,2,1,0:T(8,128)} %refs_0_.1), channel_id=1, source_target_pairs={{0,192},{32,224},{64,0},{96,32},{128,64},{160,96},{192,128},{224,1... | collective-permute-start | bytes 786440 | tf_op jit(solution)/shard_map/ppermute | solution.py:254
  5.2 0.3 collective-permute-start.5
  5.5 5.1 %collective-permute-done.3.refs_0_ = f32[4,2,8,1024]{3,2,1,0:T(8,128)S(1)} collective-permute-done((f32[4,2,8,1024]{3,2,1,0:T(8,128)}, f32[4,2,8,1024]{3,2,1,0:T(8,128)S(1)}, u32[]{:S(2)}, u32[]{:S(2)}) %collective-permute-start.3) | collective-permute-done | bytes 262176 | tf_op jit(solution)/shard_map/ppermute | solution.py:254
  10.5 3.9 %collective-permute-start.4 = (f32[4,2,8,1024]{3,2,1,0:T(8,128)S(1)}, f32[4,2,8,1024]{3,2,1,0:T(8,128)S(1)}, u32[]{:S(2)}, u32[]{:S(2)}) collective-permute-start(f32[4,2,8,1024]{3,2,1,0:T(8,128)S(1)} %collective-permute-done.3.refs_0_), channel_id=1, source_target_pairs={{0,32},{32,0},{64,96},{96,64},{128,160},{160,128},{192,224},{224,1... | collective-permute-start | bytes 786440 | tf_op jit(solution)/shard_map/ppermute | solution.py:255
  14.4 1.2 collective-permute-done.7.refs_4_
  15.7 1.5 collective-permute-start.8
  17.2 11.8 %collective-permute-done.5.refs_2_ = f32[4,2,8,1024]{3,2,1,0:T(8,128)S(1)} collective-permute-done((f32[4,2,8,1024]{3,2,1,0:T(8,128)}, f32[4,2,8,1024]{3,2,1,0:T(8,128)S(1)}, u32[]{:S(2)}, u32[]{:S(2)}) %collective-permute-start.5) | collective-permute-done | bytes 262176 | tf_op jit(solution)/shard_map/ppermute | solution.py:254
  29.0 0.5 collective-permute-start.6
  29.5 0.0 collective-permute-start
  29.5 0.7 copy-done.3
  30.2 0.7 copy-done.4
  30.9 0.7 copy-done.5
  31.5 1.9 %prepare.1 = (bf16[512,256]{1,0:T(8,128)(2,1)S(1)}, bf16[512,256]{1,0:T(8,128)(2,1)S(1)}, bf16[256,384]{1,0:T(8,128)(2,1)S(1)}) custom-call(s32[3]{0:T(128)S(1)} %compare_select_fusion.1.place, f32[9]{0:T(128)S(1)} %copy-done.4, f32[9]{0:T(128)S(1)} %copy-done.5, f32[16,16]{1,0:T(8,128)S(1)} %copy-done.3), custom_call_target="tpu_custom_call" | custom-call | flops 16777216 | bytes 1048576 | tf_op jit(solution)/shard_map/prepare/pallas_call | solution.py:102
  33.4 0.0 copy-start
  33.4 2.2 %copy-done = bf16[4,4,16,8,1024]{4,3,2,1,0:T(8,128)(2,1)S(1)} copy-done((bf16[4,4,16,8,1024]{4,3,2,1,0:T(8,128)(2,1)S(1)}, bf16[4,4,16,8,1024]{4,3,2,1,0:T(8,128)(2,1)}, u32[]{:S(2)}) %copy-start) | copy-done | bytes 4194328
  35.6 2.8 %shard_map.56 = (f32[4,96,384]{2,1,0:T(8,128)S(1)}, f32[4,96,384]{2,1,0:T(8,128)S(1)}, f32[4,96,256]{2,1,0:T(8,128)S(1)}) custom-call(s32[3]{0:T(128)S(1)} %compare_select_fusion.1.place, bf16[4,4,16,8,1024]{4,3,2,1,0:T(8,128)(2,1)S(1)} %copy-done, f32[4,2,8,1024]{3,2,1,0:T(8,128)S(1)} %collective-permute-done.3.refs_0_, ...), custom_call_target="tpu_custom_call" | custom-call | flops 805306368 | bytes 6291456 | tf_op jit(solution)/shard_map/pallas_call | solution.py:165
  38.5 5.3 %collective-permute-start.9 = (f32[4,96,384]{2,1,0:T(8,128)S(1)}, f32[4,96,384]{2,1,0:T(8,128)S(1)}, u32[]{:S(2)}, u32[]{:S(2)}) collective-permute-start(f32[4,96,384]{2,1,0:T(8,128)S(1)} %get-tuple-element.40.refs_3_), channel_id=1, source_target_pairs={{0,1},{1,0},{2,3},{3,2},{4,5},{5,4},{6,7},{7,6},{8,9},{9,8},{10,11... | collective-permute-start | bytes 1769480 | tf_op jit(solution)/shard_map/ppermute | solution.py:266
  43.8 1.4 shard_map.55.refs_0_
  45.2 0.2 collective-permute-start.1
  45.4 5.2 %collective-permute-start.15 = (f32[4,96,384]{2,1,0:T(8,128)S(1)}, f32[4,96,384]{2,1,0:T(8,128)S(1)}, u32[]{:S(2)}, u32[]{:S(2)}) collective-permute-start(f32[4,96,384]{2,1,0:T(8,128)S(1)} %get-tuple-element.51.refs_3_), channel_id=1, source_target_pairs={{0,1},{1,0},{2,3},{3,2},{4,5},{5,4},{6,7},{7,6},{8,9},{9,8},{10,11... | collective-permute-start | bytes 1769480 | tf_op jit(solution)/shard_map/ppermute | solution.py:266
  50.7 0.2 collective-permute-start.21
  50.8 21.3 %collective-permute-done.9.refs_4_ = f32[4,96,384]{2,1,0:T(8,128)S(1)} collective-permute-done((f32[4,96,384]{2,1,0:T(8,128)S(1)}, f32[4,96,384]{2,1,0:T(8,128)S(1)}, u32[]{:S(2)}, u32[]{:S(2)}) %collective-permute-start.9) | collective-permute-done | bytes 589856 | tf_op jit(solution)/shard_map/ppermute | solution.py:266
  72.1 3.2 %collective-permute-start.10 = (f32[4,96,384]{2,1,0:T(8,128)S(1)}, f32[4,96,384]{2,1,0:T(8,128)S(1)}, u32[]{:S(2)}, u32[]{:S(2)}) collective-permute-start(f32[4,96,384]{2,1,0:T(8,128)S(1)} %collective-permute-done.9.refs_4_), channel_id=1, source_target_pairs={{0,2},{2,4},{4,6},{6,8},{8,10},{10,12},{12,14},{14,16},{16,18},{18... | collective-permute-start | bytes 1769480 | tf_op jit(solution)/shard_map/ppermute | solution.py:269
  75.4 24.5 %collective-permute-done.1.refs_1_ = f32[4,32,1024]{2,1,0:T(8,128)S(1)} collective-permute-done((f32[4,32,1024]{2,1,0:T(8,128)S(1)}, f32[4,32,1024]{2,1,0:T(8,128)S(1)}, u32[]{:S(2)}, u32[]{:S(2)}) %collective-permute-start.1) | collective-permute-done | bytes 524320 | tf_op jit(solution)/shard_map/ppermute | solution.py:261
  99.9 3.2 %collective-permute-start.2 = (f32[4,32,1024]{2,1,0:T(8,128)S(1)}, f32[4,32,1024]{2,1,0:T(8,128)S(1)}, u32[]{:S(2)}, u32[]{:S(2)}) collective-permute-start(f32[4,32,1024]{2,1,0:T(8,128)S(1)} %collective-permute-done.1.refs_1_), channel_id=1, source_target_pairs={{0,2},{2,4},{4,6},{6,8},{8,10},{10,12},{12,14},{14,16},{16,18},{18... | collective-permute-start | bytes 1572872 | tf_op jit(solution)/shard_map/ppermute | solution.py:262
  103.2 23.1 %collective-permute-done.15.refs_4_ = f32[4,96,384]{2,1,0:T(8,128)S(1)} collective-permute-done((f32[4,96,384]{2,1,0:T(8,128)S(1)}, f32[4,96,384]{2,1,0:T(8,128)S(1)}, u32[]{:S(2)}, u32[]{:S(2)}) %collective-permute-start.15) | collective-permute-done | bytes 589856 | tf_op jit(solution)/shard_map/ppermute | solution.py:266
  126.3 3.2 %collective-permute-start.16 = (f32[4,96,384]{2,1,0:T(8,128)S(1)}, f32[4,96,384]{2,1,0:T(8,128)S(1)}, u32[]{:S(2)}, u32[]{:S(2)}) collective-permute-start(f32[4,96,384]{2,1,0:T(8,128)S(1)} %collective-permute-done.15.refs_4_), channel_id=1, source_target_pairs={{0,2},{2,4},{4,6},{6,8},{8,10},{10,12},{12,14},{14,16},{16,18},{18... | collective-permute-start | bytes 1769480 | tf_op jit(solution)/shard_map/ppermute | solution.py:269
  129.5 5.2 %collective-permute-done.21.refs_4_ = f32[4,96,256]{2,1,0:T(8,128)S(1)} collective-permute-done((f32[4,96,256]{2,1,0:T(8,128)S(1)}, f32[4,96,256]{2,1,0:T(8,128)S(1)}, u32[]{:S(2)}, u32[]{:S(2)}) %collective-permute-start.21) | collective-permute-done | bytes 393248 | tf_op jit(solution)/shard_map/ppermute | solution.py:266
  134.7 3.2 %collective-permute-start.22 = (f32[4,96,256]{2,1,0:T(8,128)S(1)}, f32[4,96,256]{2,1,0:T(8,128)S(1)}, u32[]{:S(2)}, u32[]{:S(2)}) collective-permute-start(f32[4,96,256]{2,1,0:T(8,128)S(1)} %collective-permute-done.21.refs_4_), channel_id=1, source_target_pairs={{0,2},{2,4},{4,6},{6,8},{8,10},{10,12},{12,14},{14,16},{16,18},{18... | collective-permute-start | bytes 1179656 | tf_op jit(solution)/shard_map/ppermute | solution.py:269
  138.0 2.2 %shard_map.57 = (f32[4,2,8,384]{3,2,1,0:T(8,128)S(1)}, f32[4,2,8,384]{3,2,1,0:T(8,128)S(1)}, f32[4,2,8,384]{3,2,1,0:T(8,128)S(1)}, f32[4,2,8,384]{3,2,1,0:T(8,128)S(1)}, f32[4,4,2,8,384]{4,3,2,1,0:T(8,128)S(1)}) custom-call(s32[3]{0:T(128)S(1)} %compare_select_fusion.1.place, bf16[4,4,16,8,1024]{4,3,2,1,0:T(8,128)(2,1)S(1)} %copy-done.1, ...), custom_call_target="tpu_custom_call" | custom-call | flops 402653184 | bytes 4718592 | tf_op jit(solution)/shard_map/pallas_call | solution.py:213
  140.2 1.8 collective-permute-start.11
  142.0 6.2 %collective-permute-done.22.refs_5_ = f32[4,96,256]{2,1,0:T(8,128)S(1)} collective-permute-done((f32[4,96,256]{2,1,0:T(8,128)S(1)}, f32[4,96,256]{2,1,0:T(8,128)S(1)}, u32[]{:S(2)}, u32[]{:S(2)}) %collective-permute-start.22) | collective-permute-done | bytes 393248 | tf_op jit(solution)/shard_map/ppermute | solution.py:269
  148.2 1.8 shard_map.59
  150.0 3.3 %collective-permute-start.23 = (f32[4,4,2,8,256]{4,3,2,1,0:T(8,128)S(1)}, f32[4,4,2,8,256]{4,3,2,1,0:T(8,128)S(1)}, u32[]{:S(2)}, u32[]{:S(2)}) collective-permute-start(f32[4,4,2,8,256]{4,3,2,1,0:T(8,128)S(1)} %get-tuple-element.66), channel_id=1, source_target_pairs={{0,32},{32,0},{64,96},{96,64},{128,160},{160,128},{192,224},{224,1... | collective-permute-start | bytes 786440 | tf_op jit(solution)/shard_map/ppermute | solution.py:273
  153.3 2.2 %shard_map.58 = (f32[4,2,8,384]{3,2,1,0:T(8,128)S(1)}, f32[4,2,8,384]{3,2,1,0:T(8,128)S(1)}, f32[4,2,8,384]{3,2,1,0:T(8,128)S(1)}, f32[4,2,8,384]{3,2,1,0:T(8,128)S(1)}, f32[4,4,2,8,384]{4,3,2,1,0:T(8,128)S(1)}) custom-call(s32[3]{0:T(128)S(1)} %compare_select_fusion.1.place, bf16[4,4,16,8,1024]{4,3,2,1,0:T(8,128)(2,1)S(1)} %copy-done.1, ...), custom_call_target="tpu_custom_call" | custom-call | flops 402653184 | bytes 4718592 | tf_op jit(solution)/shard_map/pallas_call | solution.py:213
  155.5 0.3 collective-permute-start.17
  155.9 0.1 collective-permute-start.24
  156.0 1.1 collective-permute-start.25
  157.1 2.1 %collective-permute-start.26 = (f32[4,2,8,256]{3,2,1,0:T(8,128)S(1)}, f32[4,2,8,256]{3,2,1,0:T(8,128)S(1)}, u32[]{:S(2)}, u32[]{:S(2)}) collective-permute-start(f32[4,2,8,256]{3,2,1,0:T(8,128)S(1)} %get-tuple-element.70), channel_id=1, source_target_pairs={{0,192},{32,224},{64,0},{96,32},{128,64},{160,96},{192,128},{224,1... | collective-permute-start | bytes 196616 | tf_op jit(solution)/shard_map/ppermute | solution.py:277
  159.3 0.4 collective-permute-start.12
  159.6 1.3 collective-permute-done.24
  161.0 5.0 %collective-permute-start.14 = (f32[4,2,8,384]{3,2,1,0:T(8,128)S(1)}, f32[4,2,8,384]{3,2,1,0:T(8,128)S(1)}, u32[]{:S(2)}, u32[]{:S(2)}) collective-permute-start(f32[4,2,8,384]{3,2,1,0:T(8,128)S(1)} %get-tuple-element.50), channel_id=1, source_target_pairs={{0,192},{32,224},{64,0},{96,32},{128,64},{160,96},{192,128},{224,1... | collective-permute-start | bytes 294920 | tf_op jit(solution)/shard_map/ppermute | solution.py:277
  166.1 2.5 %collective-permute-start.18 = (f32[4,2,8,384]{3,2,1,0:T(8,128)S(1)}, f32[4,2,8,384]{3,2,1,0:T(8,128)S(1)}, u32[]{:S(2)}, u32[]{:S(2)}) collective-permute-start(f32[4,2,8,384]{3,2,1,0:T(8,128)S(1)} %get-tuple-element.58), channel_id=1, source_target_pairs={{0,64},{32,96},{64,128},{96,160},{128,192},{160,224},{192,0},{224,... | collective-permute-start | bytes 294920 | tf_op jit(solution)/shard_map/ppermute | solution.py:277
  168.6 2.2 %collective-permute-start.20 = (f32[4,2,8,384]{3,2,1,0:T(8,128)S(1)}, f32[4,2,8,384]{3,2,1,0:T(8,128)S(1)}, u32[]{:S(2)}, u32[]{:S(2)}) collective-permute-start(f32[4,2,8,384]{3,2,1,0:T(8,128)S(1)} %get-tuple-element.60), channel_id=1, source_target_pairs={{0,192},{32,224},{64,0},{96,32},{128,64},{160,96},{192,128},{224,1... | collective-permute-start | bytes 294920 | tf_op jit(solution)/shard_map/ppermute | solution.py:277
  170.8 2.8 %collective-permute-done.13 = f32[4,2,8,384]{3,2,1,0:T(8,128)S(1)} collective-permute-done((f32[4,2,8,384]{3,2,1,0:T(8,128)S(1)}, f32[4,2,8,384]{3,2,1,0:T(8,128)S(1)}, u32[]{:S(2)}, u32[]{:S(2)}) %collective-permute-start.13) | collective-permute-done | bytes 98336 | tf_op jit(solution)/shard_map/ppermute | solution.py:277
  173.7 5.9 %collective-permute-done.19 = f32[4,2,8,384]{3,2,1,0:T(8,128)S(1)} collective-permute-done((f32[4,2,8,384]{3,2,1,0:T(8,128)S(1)}, f32[4,2,8,384]{3,2,1,0:T(8,128)S(1)}, u32[]{:S(2)}, u32[]{:S(2)}) %collective-permute-start.19) | collective-permute-done | bytes 98336 | tf_op jit(solution)/shard_map/ppermute | solution.py:277
  179.6 0.7 maximum_multiply_fusion
  (32 shorter events, 0.2 us)
Async XLA Ops:
  0.0 10.5 %collective-permute-start.3 = (f32[4,2,8,1024]{3,2,1,0:T(8,128)}, f32[4,2,8,1024]{3,2,1,0:T(8,128)S(1)}, u32[]{:S(2)}, u32[]{:S(2)}) collective-permute-start(f32[4,2,8,1024]{3,2,1,0:T(8,128)} %refs_0_.1), channel_id=1, source_target_pairs={{0,64},{32,96},{64,128},{96,160},{128,192},{160,224},{192,0},{224,... | collective-permute-start | bytes 786440 | tf_op jit(solution)/shard_map/ppermute | solution.py:254
  2.5 13.2 %collective-permute-start.7 = (f32[4,2,8,1024]{3,2,1,0:T(8,128)}, f32[4,2,8,1024]{3,2,1,0:T(8,128)S(1)}, u32[]{:S(2)}, u32[]{:S(2)}) collective-permute-start(f32[4,2,8,1024]{3,2,1,0:T(8,128)} %refs_0_.1), channel_id=1, source_target_pairs={{0,192},{32,224},{64,0},{96,32},{128,64},{160,96},{192,128},{224,1... | collective-permute-start | bytes 786440 | tf_op jit(solution)/shard_map/ppermute | solution.py:254
  5.2 23.8 %collective-permute-start.5 = (f32[4,2,8,1024]{3,2,1,0:T(8,128)}, f32[4,2,8,1024]{3,2,1,0:T(8,128)S(1)}, u32[]{:S(2)}, u32[]{:S(2)}) collective-permute-start(f32[4,2,8,1024]{3,2,1,0:T(8,128)} %refs_0_.1), channel_id=1, source_target_pairs={{0,128},{32,160},{64,192},{96,224},{128,0},{160,32},{192,64},{224,... | collective-permute-start | bytes 786440 | tf_op jit(solution)/shard_map/ppermute | solution.py:254
  10.5 22.9 %collective-permute-start.4 = (f32[4,2,8,1024]{3,2,1,0:T(8,128)S(1)}, f32[4,2,8,1024]{3,2,1,0:T(8,128)S(1)}, u32[]{:S(2)}, u32[]{:S(2)}) collective-permute-start(f32[4,2,8,1024]{3,2,1,0:T(8,128)S(1)} %collective-permute-done.3.refs_0_), channel_id=1, source_target_pairs={{0,32},{32,0},{64,96},{96,64},{128,160},{160,128},{192,224},{224,1... | collective-permute-start | bytes 786440 | tf_op jit(solution)/shard_map/ppermute | solution.py:255
  15.7 17.7 %collective-permute-start.8 = (f32[4,2,8,1024]{3,2,1,0:T(8,128)S(1)}, f32[4,2,8,1024]{3,2,1,0:T(8,128)S(1)}, u32[]{:S(2)}, u32[]{:S(2)}) collective-permute-start(f32[4,2,8,1024]{3,2,1,0:T(8,128)S(1)} %collective-permute-done.7.refs_4_), channel_id=1, source_target_pairs={{0,32},{32,0},{64,96},{96,64},{128,160},{160,128},{192,224},{224,1... | collective-permute-start | bytes 786440 | tf_op jit(solution)/shard_map/ppermute | solution.py:255
  29.0 4.4 %collective-permute-start.6 = (f32[4,2,8,1024]{3,2,1,0:T(8,128)S(1)}, f32[4,2,8,1024]{3,2,1,0:T(8,128)S(1)}, u32[]{:S(2)}, u32[]{:S(2)}) collective-permute-start(f32[4,2,8,1024]{3,2,1,0:T(8,128)S(1)} %collective-permute-done.5.refs_2_), channel_id=1, source_target_pairs={{0,32},{32,0},{64,96},{96,64},{128,160},{160,128},{192,224},{224,1... | collective-permute-start | bytes 786440 | tf_op jit(solution)/shard_map/ppermute | solution.py:255
  29.5 14.3 %collective-permute-start = (f32[4,2,8,1024]{3,2,1,0:T(8,128)}, f32[4,2,8,1024]{3,2,1,0:T(8,128)S(1)}, u32[]{:S(2)}, u32[]{:S(2)}) collective-permute-start(f32[4,2,8,1024]{3,2,1,0:T(8,128)} %refs_0_.1), channel_id=1, source_target_pairs={{0,32},{32,0},{64,96},{96,64},{128,160},{160,128},{192,224},{224,1... | collective-permute-start | bytes 786440 | tf_op jit(solution)/shard_map/ppermute | solution.py:255
  29.5 0.7 copy-start.3
  30.2 0.7 copy-start.4
  30.9 0.7 copy-start.5
  33.4 2.2 %copy-start = (bf16[4,4,16,8,1024]{4,3,2,1,0:T(8,128)(2,1)S(1)}, bf16[4,4,16,8,1024]{4,3,2,1,0:T(8,128)(2,1)}, u32[]{:S(2)}) copy-start(bf16[4,4,16,8,1024]{4,3,2,1,0:T(8,128)(2,1)} %members.9) | copy-start | bytes 12582916
  35.6 8.2 %copy-start.2 = (f32[4,2,8,1024]{3,2,1,0:T(8,128)S(1)}, f32[4,2,8,1024]{3,2,1,0:T(8,128)}, u32[]{:S(2)}) copy-start(f32[4,2,8,1024]{3,2,1,0:T(8,128)} %refs_0_.1) | copy-start | bytes 786436
  38.5 99.5 %copy-start.1 = (bf16[4,4,16,8,1024]{4,3,2,1,0:T(8,128)(2,1)S(1)}, bf16[4,4,16,8,1024]{4,3,2,1,0:T(8,128)(2,1)}, u32[]{:S(2)}) copy-start(bf16[4,4,16,8,1024]{4,3,2,1,0:T(8,128)(2,1)} %members.9) | copy-start | bytes 12582916
  38.5 33.6 %collective-permute-start.9 = (f32[4,96,384]{2,1,0:T(8,128)S(1)}, f32[4,96,384]{2,1,0:T(8,128)S(1)}, u32[]{:S(2)}, u32[]{:S(2)}) collective-permute-start(f32[4,96,384]{2,1,0:T(8,128)S(1)} %get-tuple-element.40.refs_3_), channel_id=1, source_target_pairs={{0,1},{1,0},{2,3},{3,2},{4,5},{5,4},{6,7},{7,6},{8,9},{9,8},{10,11... | collective-permute-start | bytes 1769480 | tf_op jit(solution)/shard_map/ppermute | solution.py:266
  45.2 54.7 %collective-permute-start.1 = (f32[4,32,1024]{2,1,0:T(8,128)S(1)}, f32[4,32,1024]{2,1,0:T(8,128)S(1)}, u32[]{:S(2)}, u32[]{:S(2)}) collective-permute-start(f32[4,32,1024]{2,1,0:T(8,128)S(1)} %shard_map.55.refs_0_), channel_id=1, source_target_pairs={{0,1},{1,0},{2,3},{3,2},{4,5},{5,4},{6,7},{7,6},{8,9},{9,8},{10,11... | collective-permute-start | bytes 1572872 | tf_op jit(solution)/shard_map/ppermute | solution.py:261
  45.4 80.8 %collective-permute-start.15 = (f32[4,96,384]{2,1,0:T(8,128)S(1)}, f32[4,96,384]{2,1,0:T(8,128)S(1)}, u32[]{:S(2)}, u32[]{:S(2)}) collective-permute-start(f32[4,96,384]{2,1,0:T(8,128)S(1)} %get-tuple-element.51.refs_3_), channel_id=1, source_target_pairs={{0,1},{1,0},{2,3},{3,2},{4,5},{5,4},{6,7},{7,6},{8,9},{9,8},{10,11... | collective-permute-start | bytes 1769480 | tf_op jit(solution)/shard_map/ppermute | solution.py:266
  50.7 84.0 %collective-permute-start.21 = (f32[4,96,256]{2,1,0:T(8,128)S(1)}, f32[4,96,256]{2,1,0:T(8,128)S(1)}, u32[]{:S(2)}, u32[]{:S(2)}) collective-permute-start(f32[4,96,256]{2,1,0:T(8,128)S(1)} %get-tuple-element.61.refs_3_), channel_id=1, source_target_pairs={{0,1},{1,0},{2,3},{3,2},{4,5},{5,4},{6,7},{7,6},{8,9},{9,8},{10,11... | collective-permute-start | bytes 1179656 | tf_op jit(solution)/shard_map/ppermute | solution.py:266
  72.1 65.9 %collective-permute-start.10 = (f32[4,96,384]{2,1,0:T(8,128)S(1)}, f32[4,96,384]{2,1,0:T(8,128)S(1)}, u32[]{:S(2)}, u32[]{:S(2)}) collective-permute-start(f32[4,96,384]{2,1,0:T(8,128)S(1)} %collective-permute-done.9.refs_4_), channel_id=1, source_target_pairs={{0,2},{2,4},{4,6},{6,8},{8,10},{10,12},{12,14},{14,16},{16,18},{18... | collective-permute-start | bytes 1769480 | tf_op jit(solution)/shard_map/ppermute | solution.py:269
  99.9 38.1 %collective-permute-start.2 = (f32[4,32,1024]{2,1,0:T(8,128)S(1)}, f32[4,32,1024]{2,1,0:T(8,128)S(1)}, u32[]{:S(2)}, u32[]{:S(2)}) collective-permute-start(f32[4,32,1024]{2,1,0:T(8,128)S(1)} %collective-permute-done.1.refs_1_), channel_id=1, source_target_pairs={{0,2},{2,4},{4,6},{6,8},{8,10},{10,12},{12,14},{14,16},{16,18},{18... | collective-permute-start | bytes 1572872 | tf_op jit(solution)/shard_map/ppermute | solution.py:262
  126.3 27.0 %collective-permute-start.16 = (f32[4,96,384]{2,1,0:T(8,128)S(1)}, f32[4,96,384]{2,1,0:T(8,128)S(1)}, u32[]{:S(2)}, u32[]{:S(2)}) collective-permute-start(f32[4,96,384]{2,1,0:T(8,128)S(1)} %collective-permute-done.15.refs_4_), channel_id=1, source_target_pairs={{0,2},{2,4},{4,6},{6,8},{8,10},{10,12},{12,14},{14,16},{16,18},{18... | collective-permute-start | bytes 1769480 | tf_op jit(solution)/shard_map/ppermute | solution.py:269
  134.7 13.5 %collective-permute-start.22 = (f32[4,96,256]{2,1,0:T(8,128)S(1)}, f32[4,96,256]{2,1,0:T(8,128)S(1)}, u32[]{:S(2)}, u32[]{:S(2)}) collective-permute-start(f32[4,96,256]{2,1,0:T(8,128)S(1)} %collective-permute-done.21.refs_4_), channel_id=1, source_target_pairs={{0,2},{2,4},{4,6},{6,8},{8,10},{10,12},{12,14},{14,16},{16,18},{18... | collective-permute-start | bytes 1179656 | tf_op jit(solution)/shard_map/ppermute | solution.py:269
  140.2 19.0 %collective-permute-start.11 = (f32[4,4,2,8,384]{4,3,2,1,0:T(8,128)S(1)}, f32[4,4,2,8,384]{4,3,2,1,0:T(8,128)S(1)}, u32[]{:S(2)}, u32[]{:S(2)}) collective-permute-start(f32[4,4,2,8,384]{4,3,2,1,0:T(8,128)S(1)} %get-tuple-element.46), channel_id=1, source_target_pairs={{0,32},{32,0},{64,96},{96,64},{128,160},{160,128},{192,224},{224,1... | collective-permute-start | bytes 1179656 | tf_op jit(solution)/shard_map/ppermute | solution.py:273
  150.0 5.8 %collective-permute-start.23 = (f32[4,4,2,8,256]{4,3,2,1,0:T(8,128)S(1)}, f32[4,4,2,8,256]{4,3,2,1,0:T(8,128)S(1)}, u32[]{:S(2)}, u32[]{:S(2)}) collective-permute-start(f32[4,4,2,8,256]{4,3,2,1,0:T(8,128)S(1)} %get-tuple-element.66), channel_id=1, source_target_pairs={{0,32},{32,0},{64,96},{96,64},{128,160},{160,128},{192,224},{224,1... | collective-permute-start | bytes 786440 | tf_op jit(solution)/shard_map/ppermute | solution.py:273
  155.5 10.5 %collective-permute-start.17 = (f32[4,4,2,8,384]{4,3,2,1,0:T(8,128)S(1)}, f32[4,4,2,8,384]{4,3,2,1,0:T(8,128)S(1)}, u32[]{:S(2)}, u32[]{:S(2)}) collective-permute-start(f32[4,4,2,8,384]{4,3,2,1,0:T(8,128)S(1)} %get-tuple-element.56), channel_id=1, source_target_pairs={{0,32},{32,0},{64,96},{96,64},{128,160},{160,128},{192,224},{224,1... | collective-permute-start | bytes 1179656 | tf_op jit(solution)/shard_map/ppermute | solution.py:273
  155.9 5.1 %collective-permute-start.24 = (f32[4,2,8,256]{3,2,1,0:T(8,128)S(1)}, f32[4,2,8,256]{3,2,1,0:T(8,128)S(1)}, u32[]{:S(2)}, u32[]{:S(2)}) collective-permute-start(f32[4,2,8,256]{3,2,1,0:T(8,128)S(1)} %get-tuple-element.68), channel_id=1, source_target_pairs={{0,64},{32,96},{64,128},{96,160},{128,192},{160,224},{192,0},{224,... | collective-permute-start | bytes 196616 | tf_op jit(solution)/shard_map/ppermute | solution.py:277
  156.0 5.0 %collective-permute-start.25 = (f32[4,2,8,256]{3,2,1,0:T(8,128)S(1)}, f32[4,2,8,256]{3,2,1,0:T(8,128)S(1)}, u32[]{:S(2)}, u32[]{:S(2)}) collective-permute-start(f32[4,2,8,256]{3,2,1,0:T(8,128)S(1)} %get-tuple-element.69), channel_id=1, source_target_pairs={{0,128},{32,160},{64,192},{96,224},{128,0},{160,32},{192,64},{224,... | collective-permute-start | bytes 196616 | tf_op jit(solution)/shard_map/ppermute | solution.py:277
  157.1 8.9 %collective-permute-start.26 = (f32[4,2,8,256]{3,2,1,0:T(8,128)S(1)}, f32[4,2,8,256]{3,2,1,0:T(8,128)S(1)}, u32[]{:S(2)}, u32[]{:S(2)}) collective-permute-start(f32[4,2,8,256]{3,2,1,0:T(8,128)S(1)} %get-tuple-element.70), channel_id=1, source_target_pairs={{0,192},{32,224},{64,0},{96,32},{128,64},{160,96},{192,128},{224,1... | collective-permute-start | bytes 196616 | tf_op jit(solution)/shard_map/ppermute | solution.py:277
  159.3 9.4 %collective-permute-start.12 = (f32[4,2,8,384]{3,2,1,0:T(8,128)S(1)}, f32[4,2,8,384]{3,2,1,0:T(8,128)S(1)}, u32[]{:S(2)}, u32[]{:S(2)}) collective-permute-start(f32[4,2,8,384]{3,2,1,0:T(8,128)S(1)} %get-tuple-element.48), channel_id=1, source_target_pairs={{0,64},{32,96},{64,128},{96,160},{128,192},{160,224},{192,0},{224,... | collective-permute-start | bytes 294920 | tf_op jit(solution)/shard_map/ppermute | solution.py:277
  161.0 12.7 %collective-permute-start.13 = (f32[4,2,8,384]{3,2,1,0:T(8,128)S(1)}, f32[4,2,8,384]{3,2,1,0:T(8,128)S(1)}, u32[]{:S(2)}, u32[]{:S(2)}) collective-permute-start(f32[4,2,8,384]{3,2,1,0:T(8,128)S(1)} %get-tuple-element.49), channel_id=1, source_target_pairs={{0,128},{32,160},{64,192},{96,224},{128,0},{160,32},{192,64},{224,... | collective-permute-start | bytes 294920 | tf_op jit(solution)/shard_map/ppermute | solution.py:277
  161.0 12.7 %collective-permute-start.14 = (f32[4,2,8,384]{3,2,1,0:T(8,128)S(1)}, f32[4,2,8,384]{3,2,1,0:T(8,128)S(1)}, u32[]{:S(2)}, u32[]{:S(2)}) collective-permute-start(f32[4,2,8,384]{3,2,1,0:T(8,128)S(1)} %get-tuple-element.50), channel_id=1, source_target_pairs={{0,192},{32,224},{64,0},{96,32},{128,64},{160,96},{192,128},{224,1... | collective-permute-start | bytes 294920 | tf_op jit(solution)/shard_map/ppermute | solution.py:277
  166.1 7.6 %collective-permute-start.18 = (f32[4,2,8,384]{3,2,1,0:T(8,128)S(1)}, f32[4,2,8,384]{3,2,1,0:T(8,128)S(1)}, u32[]{:S(2)}, u32[]{:S(2)}) collective-permute-start(f32[4,2,8,384]{3,2,1,0:T(8,128)S(1)} %get-tuple-element.58), channel_id=1, source_target_pairs={{0,64},{32,96},{64,128},{96,160},{128,192},{160,224},{192,0},{224,... | collective-permute-start | bytes 294920 | tf_op jit(solution)/shard_map/ppermute | solution.py:277
  168.6 10.9 %collective-permute-start.19 = (f32[4,2,8,384]{3,2,1,0:T(8,128)S(1)}, f32[4,2,8,384]{3,2,1,0:T(8,128)S(1)}, u32[]{:S(2)}, u32[]{:S(2)}) collective-permute-start(f32[4,2,8,384]{3,2,1,0:T(8,128)S(1)} %get-tuple-element.59), channel_id=1, source_target_pairs={{0,128},{32,160},{64,192},{96,224},{128,0},{160,32},{192,64},{224,... | collective-permute-start | bytes 294920 | tf_op jit(solution)/shard_map/ppermute | solution.py:277
  168.6 10.9 %collective-permute-start.20 = (f32[4,2,8,384]{3,2,1,0:T(8,128)S(1)}, f32[4,2,8,384]{3,2,1,0:T(8,128)S(1)}, u32[]{:S(2)}, u32[]{:S(2)}) collective-permute-start(f32[4,2,8,384]{3,2,1,0:T(8,128)S(1)} %get-tuple-element.60), channel_id=1, source_target_pairs={{0,192},{32,224},{64,0},{96,32},{128,64},{160,96},{192,128},{224,1... | collective-permute-start | bytes 294920 | tf_op jit(solution)/shard_map/ppermute | solution.py:277
